TPU v7x, 32 devices: a whole 2x2x4 slice. The times are simulated.
32 devices in a mesh: group: 2 (over y), frame: 8 (over z, x), row: 2 (over core).
Axes of the slice: x: 2, y: 2, z: 4, core: 2. Of those that a mesh axis runs over, the one named last changes fastest.
Arguments:
- latents: bfloat16 [16, 8, 32, 1120], P(('group', 'frame'), 'row'), parts along dimension 0, may hold values from -24 to 24
- spatial_weights: bfloat16 [4, 10, 112, 112], replicated, may hold values from -0.5 to 0.5
- causal_weights: bfloat16 [4, 10, 112, 112], replicated, may hold values from -0.5 to 0.5
Outputs:
- updated_latents: bfloat16 [16, 8, 32, 1120], P(('group', 'frame'), None, None, 'row'), parts along dimension 0
There are 2 independent parts, one for each index of `group`. A program takes and returns all parts, laid end to end along the dimension named above; an argument that names none is the same for every part. Nothing has to cross between parts.
All inputs are finite; a program needn't handle non-finite values.
Results may differ from a plain program's by a relative error of at most 0.0047.
The roundings to bfloat16 on the way count: a program that leaves them out, or rounds other values in their place, can miss the bound.
Values may be sent and summed in bfloat16 or wider, within the bound.
No kernel may reach another device: no remote copies, remote signals or barrier semaphores. Data moves between devices by JAX's collectives and lax.ppermute only.
A program may use at most 64 MiB of HBM per device.

v0:
```python
import jax
import jax.numpy as jnp
from jax import lax
from jax.sharding import PartitionSpec as P


def prefix(x, axis, join, neutral):
    place = lax.axis_index(axis)
    gathered = lax.all_gather(x.astype(jnp.bfloat16), axis)
    state = jnp.zeros_like(x) + jnp.asarray(neutral, x.dtype)

    def one(turn, state):
        return join(state, lax.dynamic_index_in_dim(gathered, turn, 0, False).astype(x.dtype))

    return lax.fori_loop(0, place, one, state)


def normalize(frame_block):
    feat_width = frame_block.shape[-1]
    flat_rows = frame_block.reshape(-1, feat_width).astype(jnp.float32)
    normed = flat_rows * lax.rsqrt(jnp.mean(flat_rows * flat_rows, axis=-1, keepdims=True) + 1e-06)
    return normed.astype(jnp.bfloat16).reshape(frame_block.shape)


def project(normed, weights):
    head_count = weights.shape[1]
    head_size = weights.shape[2]
    normed = normed.reshape(-1, head_count, head_size)
    mapped = jnp.einsum("thd,khde->kthe", normed, weights, preferred_element_type=jnp.float32)
    queries = jax.nn.relu(mapped[0]).astype(jnp.bfloat16)
    key_rows = jax.nn.relu(mapped[1]).astype(jnp.bfloat16)
    value_rows = mapped[2].astype(jnp.bfloat16)
    gating = jax.nn.sigmoid(mapped[3])
    return (queries, key_rows, value_rows, gating)


def local_state(key_rows, value_rows):
    return jnp.einsum("thd,the->hde", key_rows, value_rows, preferred_element_type=jnp.float32)


def attend(queries, state):
    return jnp.einsum(
        "thd,hde->the", queries.astype(jnp.float32), state, precision=lax.Precision.HIGHEST
    )


def finish(frame_block, gating, attended):
    inv_rms = lax.rsqrt(jnp.mean(attended * attended, axis=-1, keepdims=True) + 1e-05)
    branch = (gating * attended * inv_rms).reshape(frame_block.shape)
    return (frame_block.astype(jnp.float32) + branch).astype(jnp.bfloat16)


def add_states(earlier, later):
    return earlier + later


def body(latents, spatial_weights, causal_weights):
    queries, key_rows, value_rows, gating = project(normalize(latents), spatial_weights)
    frame_state = lax.psum(local_state(key_rows, value_rows), "row")
    mixed_video = finish(latents, gating, attend(queries, frame_state))
    normed_c = normalize(mixed_video)
    mixed_heads, normed_heads = (
        lax.all_to_all(mixed_video, "row", split_axis=3, concat_axis=1, tiled=True),
        lax.all_to_all(normed_c, "row", split_axis=3, concat_axis=1, tiled=True),
    )
    head_part = causal_weights.shape[1] // lax.axis_size("row")
    head_start = lax.axis_index("row") * head_part
    local_weights = lax.dynamic_slice_in_dim(causal_weights, head_start, head_part, 1)
    queries, key_rows, value_rows, gating = project(normed_heads, local_weights)
    own_state = local_state(key_rows, value_rows)
    flat_state = own_state.reshape(-1, 128)
    earlier_flat = prefix(flat_state, "frame", add_states, jnp.zeros_like(flat_state))
    earlier = earlier_flat.reshape(own_state.shape)
    attended = attend(queries, earlier + own_state)
    return finish(mixed_heads, gating, attended)


def solution(mesh):
    in_specs = (P(("group", "frame"), "row", None, None), P(), P())
    out_specs = P(("group", "frame"), None, None, "row")
    return jax.shard_map(body, mesh=mesh, in_specs=in_specs, out_specs=out_specs, check_vma=False)
```

profile of v0, /device:TPU:27, one launch (start us, length us, event | category | flops | bytes accessed | tf_op | source)
XLA Modules:
  0.0 119.3 jit_solution(12640229504760504047)
XLA Ops:
  6.5 1.6 %reshape.152 = f32[128,10,112]{2,1,0:T(8,128)S(1)} reshape(bf16[1,4,32,1120]{3,2,1,0:T(8,128)(2,1)} %param.5) | data formatting | bytes 860160 | tf_op jit(solution)/shard_map/convert_element_type | solution.py:20
  8.2 1.1 multiply_reduce_fusion
  10.1 1.1 fusion.24
  11.3 20.5 %all-reduce.2.cloned.1.call-done = f32[10,112,112]{2,1,0:T(8,128)} async-done(((f32[10,112,112]{2,1,0:T(8,128)}), f32[10,112,112]{2,1,0:T(8,128)}) %all-reduce.2.cloned.1.call-update) | async-done | bytes 501776 | tf_op jit(solution)/shard_map/psum | solution.py:59
  31.8 1.7 %multiply_reduce_fusion.2 = (f32[128,10]{0,1:T(8,128)S(1)}, f32[128,10,112]{0,2,1:T(8,128)S(1)}) fusion(f32[10,112,112]{2,1,0:T(8,128)} %all-reduce.2.cloned.1.call-done, f32[4,128,10,112]{1,3,0,2:T(8,128)S(1)} %convolution_bitcast_fusion.1), kind=kOutput, calls=%fused_computation.40 | convolution fusion | flops 193391360 | bytes 1367040 | tf_op jit(solution)/shard_map/thd,hde->the/dot_general | solution.py:42
  33.5 1.0 fusion.18
  34.5 1.6 %copy.24 = f32[128,10,112]{2,1,0:T(8,128)S(1)} copy(f32[128,10,112]{0,2,1:T(8,128)} %fusion.18) | data formatting | bytes 1146880 | tf_op jit(solution)/shard_map/mul | solution.py:49
  36.6 1.4 %copy.25 = bf16[1,4,32,1120]{2,1,0,3:T(4,128)(2,1)S(1)} copy(bf16[1,4,32,1120]{3,2,1,0:T(8,128)(2,1)S(1)} %get-tuple-element.38) | data formatting | bytes 573440 | tf_op jit(solution)/shard_map/convert_element_type | solution.py:50
  38.8 2.2 %copy.28 = bf16[1,4,32,1120]{2,1,0,3:T(4,128)(2,1)S(1)} copy(bf16[1,4,32,1120]{3,2,1,0:T(8,128)(2,1)} %fusion.2) | data formatting | bytes 573440 | tf_op jit(solution)/shard_map/convert_element_type | solution.py:22
  41.0 1.8 %reshape.159 = bf16[2,2,35840]{2,1,0:T(2,128)(2,1)} reshape(bf16[1120,1,4,32]{3,2,1,0:T(4,128)(2,1)S(1)} %bitcast.72) | data formatting | bytes 573440
  42.8 5.7 %all_to_all.24 = bf16[2,2,35840]{2,1,0:T(2,128)(2,1)} all-to-all(bf16[2,2,35840]{2,1,0:T(2,128)(2,1)} %reshape.159), channel_id=1, replica_groups=mesh['group'=2,'frame'=8,'row'=2] {'row'}, dimensions={0} | all-to-all | bytes 573440 | tf_op jit(solution)/shard_map/all_to_all | solution.py:64
  48.5 1.7 %reshape.160 = bf16[1120,1,4,32]{3,2,1,0:T(4,128)(2,1)S(1)} reshape(bf16[2,2,35840]{2,1,0:T(2,128)(2,1)} %all_to_all.24) | data formatting | bytes 573440
  50.2 1.4 %copy.29 = bf16[1,4,32,2,560]{4,2,1,3,0:T(8,128)(2,1)} copy(bf16[1,4,32,2,560]{2,1,4,3,0:T(4,128)(2,1)S(1)} %bitcast.73) | data formatting | bytes 573440 | tf_op jit(solution)/shard_map/all_to_all | solution.py:64
  51.5 1.4 %reshape.148 = bf16[256,5,112]{2,1,0:T(8,128)(2,1)S(1)} reshape(bf16[1,2,4,32,560]{4,3,2,1,0:T(8,128)(2,1)} %bitcast.76) | data formatting | bytes 573440 | tf_op jit(solution)/shard_map/reshape | solution.py:28
  52.9 1.6 %convolution_bitcast_fusion = f32[4,256,5,112]{1,3,0,2:T(8,128)S(1)} fusion(bf16[256,5,112,1]{2,1,0,3:T(8,128)(2,1)S(1)} %bitcast.75, bf16[4,10,112,112]{3,2,1,0:T(8,128)(2,1)} %param.7, s32[]{:T(128)S(6)} %select_n.7), kind=kOutput, calls=%fused_computation.1 | convolution fusion | flops 128450560 | bytes 3153924 | tf_op jit(solution)/shard_map/thd,khde->kthe/dot_general | solution.py:29
  54.5 1.4 %copy-done.1 = f32[4,256,5,112]{1,3,0,2:T(8,128)} copy-done((f32[4,256,5,112]{1,3,0,2:T(8,128)}, f32[4,256,5,112]{1,3,0,2:T(8,128)S(1)}, u32[]{:S(2)}) %copy-start.1) | copy-done | bytes 2293784
  56.4 28.5 %all_gather.4 = bf16[8,490,128]{2,1,0:T(8,128)(2,1)} all-gather(bf16[1,490,128]{2,1,0:T(8,128)(2,1)S(1)} %convert_element_type.131), channel_id=1, replica_groups=mesh['group'=2,'frame'=8,'row'=2] {'frame'}, dimensions={0}, use_global_device_ids=true | all-gather | bytes 1128960 | tf_op jit(solution)/shard_map/all_gather | solution.py:9
  84.9 6.8 %while.10 = (s32[]{:T(128)}, f32[490,128]{1,0:T(8,128)S(1)}, s32[]{:T(128)}, bf16[8,490,128]{2,1,0:T(8,128)(2,1)}, s32[]{:T(128)}, /*index=5*/s32[]{:T(128)}, s32[]{:T(128)}) while((s32[]{:T(128)}, f32[490,128]{1,0:T(8,128)S(1)}, s32[]{:T(128)}, bf16[8,490,128]{2,1,0:T(8,128)(2,1)}, s32[]{:T(128)}, /*index=5*/s32[]{:T(128)}, s32[]{:T(128)}) %tuple.22), condition=%wide.region_5.6_spmd, body=%wide.region_4.5_spmd.sunk | while | flops 125445 | bytes 627315 | solution.py:15
  85.0 0.9 convert_add_fusion.2
  85.9 0.9 convert_add_fusion.2
  86.9 0.9 convert_add_fusion.2
  87.9 0.9 convert_add_fusion.2
  88.8 0.9 convert_add_fusion.2
  89.8 0.9 convert_add_fusion.2
  90.8 0.9 convert_add_fusion.2
  91.9 1.5 %multiply_reduce_fusion.1 = (f32[256,5]{0,1:T(8,128)S(1)}, f32[256,5,112]{0,2,1:T(8,128)S(1)}) fusion(f32[4,256,5,112]{1,3,0,2:T(8,128)} %copy-done.1, f32[5,112,112]{2,1,0:T(8,128)S(1)} %reshape.149, f32[5,112,112]{2,1,0:T(8,128)S(1)} %get-tuple-element.42), kind=kOutput, calls=%fused_computation.39 | convolution fusion | flops 193454080 | bytes 1367040 | tf_op jit(solution)/shard_map/thd,hde->the/dot_general | solution.py:42
  93.5 2.0 %fusion.10 = f32[256,5,112]{0,2,1:T(8,128)} fusion(f32[256,5,112]{0,2,1:T(8,128)S(1)} %get-tuple-element.44, f32[4,256,5,112]{1,3,0,2:T(8,128)} %copy-done.1, f32[256,5]{0,1:T(8,128)S(1)} %add_rsqrt_fusion), kind=kLoop, calls=%fused_computation.25 | loop fusion | flops 716800 | bytes 1725440 | tf_op jit(solution)/shard_map/mul | solution.py:49
  95.5 1.5 %copy.32 = f32[256,5,112]{2,1,0:T(8,128)S(1)} copy(f32[256,5,112]{0,2,1:T(8,128)} %fusion.10) | data formatting | bytes 1146880 | tf_op jit(solution)/shard_map/mul | solution.py:49
  97.0 1.1 reshape.150
  98.0 1.1 reshape.157
  99.2 10.2 %all_to_all.25 = bf16[2,2,35840]{2,1,0:T(2,128)(2,1)S(1)} all-to-all(bf16[2,2,35840]{2,1,0:T(2,128)(2,1)S(1)} %reshape.157), channel_id=1, replica_groups=mesh['group'=2,'frame'=8,'row'=2] {'row'}, dimensions={0} | all-to-all | bytes 573440 | tf_op jit(solution)/shard_map/all_to_all | solution.py:63
  110.6 1.9 %add_convert_fusion = bf16[1,8,32,560]{3,2,1,0:T(8,128)(2,1)} fusion(f32[1,8,32,560]{3,2,1,0:T(8,128)S(1)} %bitcast.74, f32[1,8,32,560]{3,2,1,0:T(8,128)} %reshape.150), kind=kLoop, calls=%fused_computation.9 | loop fusion | flops 286720 | bytes 1433600 | tf_op jit(solution)/shard_map/convert_element_type | solution.py:50
  (23 shorter events, 4.1 us)
Async XLA Ops:
  6.5 3.1 %copy-start = (bf16[4,10,112,112]{3,2,1,0:T(8,128)(2,1)S(1)}, bf16[4,10,112,112]{3,2,1,0:T(8,128)(2,1)}, u32[]{:S(2)}) copy-start(bf16[4,10,112,112]{3,2,1,0:T(8,128)(2,1)} %param.6) | copy-start | bytes 3010564
  6.5 25.2 %all-reduce.2.cloned.1.call-start = ((), (), s32[]{:S(2)}) async-start(), calls=%async_computation.2 | async-start | bytes 1146880 | tf_op jit(solution)/shard_map/psum | solution.py:59
  34.5 1.9 %copy-start.2 = (bf16[1,4,32,1120]{3,2,1,0:T(8,128)(2,1)S(1)}, bf16[1,4,32,1120]{3,2,1,0:T(8,128)(2,1)}, u32[]{:S(2)}) copy-start(bf16[1,4,32,1120]{3,2,1,0:T(8,128)(2,1)} %param.5) | copy-start | bytes 860164
  54.5 1.4 %copy-start.1 = (f32[4,256,5,112]{1,3,0,2:T(8,128)}, f32[4,256,5,112]{1,3,0,2:T(8,128)S(1)}, u32[]{:S(2)}) copy-start(f32[4,256,5,112]{1,3,0,2:T(8,128)S(1)} %convolution_bitcast_fusion) | copy-start | bytes 6881284
Sparse Core Ops, SparseCore 0:
  11.4 20.3 all-reduce.1
where the time goes:
time: 120 us; the launch traced here: 119 us
  blocking collectives  44.3 us (37%)
  waiting for transfers between devices  20.5 us (17%)
  local copies, waits for them, and re-layouts  20.2 us (17%)
  other arithmetic  13.8 us (12%)
  between operations  13.6 us (11%)
  matrix products  6.67 us (6%)
    all_gather x1, blocking collectives, prefix(): gathered = lax.all_gather(x.astype(jnp.bfloat16), axis)  28.5 us
    psum x1, waiting for transfers between devices, body(): frame_state = lax.psum(local_state(key_rows, value_rows), 'row')  20.5 us
    all_to_all x1, blocking collectives, body(): lax.all_to_all(mixed_video, 'row', split_axis=3, concat_axis=1, tiled=True)  10.2 us
    add x7, other arithmetic, add_states(): return earlier + later  6.6 us
    unnamed x10, local copies, waits for them, and re-layouts  6.55 us
    all_to_all x1, blocking collectives, body(): lax.all_to_all(normed_c, 'row', split_axis=3, concat_axis=1, tiled=True)  5.67 us
    dot_general x2, matrix products, attend(): jnp.einsum('thd,hde->the', queries.astype(jnp.float32), state, precision=...  3.21 us
    mul x2, local copies, waits for them, and re-layouts, finish(): branch = (gating * attended * inv_rms).reshape(frame_block.shape)  3.07 us
  transfers between devices with their start and end apart: 1, of which 1 were waited for; matrix products, arithmetic and copies ran while one was open for 0% of the time, Pallas kernels for 0%

commit v1 on v0

v1 whole, which is shorter than its diff:
```python
import functools

import jax
import jax.numpy as jnp
from jax import lax
from jax.experimental import pallas as pl
from jax.experimental.pallas import tpu as pltpu
from jax.sharding import PartitionSpec as P

LANES = 128
F32 = jnp.float32
BF16 = jnp.bfloat16
VMEM = pl.BlockSpec(memory_space=pltpu.VMEM)
SMEM = pl.BlockSpec(memory_space=pltpu.SMEM)


def call(kernel, name, out_shape, operands, in_specs, scratch=(), flops=0, limit=24 << 20):
    n_bytes = sum(o.size * o.dtype.itemsize for o in operands)
    n_bytes += sum(o.size * o.dtype.itemsize for o in out_shape)
    return pl.pallas_call(
        kernel,
        name=name,
        out_shape=tuple(out_shape),
        in_specs=in_specs,
        out_specs=tuple(VMEM for _ in out_shape),
        scratch_shapes=list(scratch),
        compiler_params=pltpu.CompilerParams(vmem_limit_bytes=limit),
        cost_estimate=pl.CostEstimate(flops=flops, bytes_accessed=n_bytes, transcendentals=0),
    )(*operands)


def pack_kernel(heads, row_ref, *refs):
    half = len(refs) // 2
    first = row_ref[0] * heads
    for w_ref, out_ref in zip(refs[:half], refs[half:]):
        maps, dim = w_ref.shape[0], w_ref.shape[2]
        out_ref[...] = jnp.zeros_like(out_ref)
        for h in range(heads):
            for m in range(maps):
                out_ref[h, :dim, m * LANES : m * LANES + dim] = w_ref[m, first + h]


def spatial_kernel(heads, dim, n_row, row_ref, own_ref, other_ref, w_ref, mixed_ref, part_ref, x_ref, inv_ref):
    band, width = own_ref.shape
    row = row_ref[0]
    x_ref[...] = jnp.zeros_like(x_ref)
    for src, place in ((own_ref, row), (other_ref, n_row - 1 - row)):
        at = pl.ds(pl.multiple_of(place * band, band), band)
        full = src[...].astype(F32)
        inv = lax.rsqrt(jnp.sum(full * full, axis=-1, keepdims=True) / width + 1e-06)
        inv_ref[at, :] = jnp.broadcast_to(inv, (band, LANES))
        for r in range(n_row):

            @pl.when(row == r)
            def _():
                for h in range(heads):
                    lo = (r * heads + h) * dim
                    x_ref[h, at, :dim] = src[:, lo : lo + dim]

    inv = inv_ref[...]
    part = jnp.zeros(part_ref.shape, F32)
    for h in range(heads):
        x = x_ref[h].astype(F32)
        u = (x * inv).astype(BF16)
        mapped = jnp.dot(u, w_ref[h], preferred_element_type=F32)
        q = jnp.maximum(mapped[:, :LANES], 0.0).astype(BF16)
        k = jnp.maximum(mapped[:, LANES : 2 * LANES], 0.0).astype(BF16)
        v = mapped[:, 2 * LANES : 3 * LANES].astype(BF16)
        gate = jax.nn.sigmoid(mapped[:, 3 * LANES :])
        state = lax.dot_general(k, v, (((0,), (0,)), ((), ())), preferred_element_type=F32)
        mixed = finish(x, gate, attend(q, state), dim)
        mixed_ref[h] = mixed
        wide = mixed.astype(F32)
        part = part + wide * wide
    part_ref[...] = part


def attend(q, state):
    high = state.astype(BF16)
    low = (state - high.astype(F32)).astype(BF16)
    return jnp.dot(
        jnp.concatenate([q, q], axis=1),
        jnp.concatenate([high, low], axis=0),
        preferred_element_type=F32,
    )


def finish(x, gate, attended, dim):
    inv_rms = lax.rsqrt(jnp.sum(attended * attended, axis=-1, keepdims=True) / dim + 1e-05)
    return (x + gate * attended * inv_rms).astype(BF16)


def state_kernel(heads, dim, width, mixed_ref, part_ref, part_other_ref, w_ref, normed_ref, state_ref, sent_ref):
    total = jnp.sum(part_ref[...] + part_other_ref[...], axis=-1, keepdims=True)
    inv = lax.rsqrt(total / width + 1e-06)
    for h in range(heads):
        u = (mixed_ref[h].astype(F32) * inv).astype(BF16)
        normed_ref[h] = u
        mapped = jnp.dot(u, w_ref[h, :, LANES : 3 * LANES], preferred_element_type=F32)
        k = jnp.maximum(mapped[:, :LANES], 0.0).astype(BF16)
        v = mapped[:, LANES:].astype(BF16)
        state = lax.dot_general(k, v, (((0,), (0,)), ((), ())), preferred_element_type=F32)
        state_ref[h * dim : (h + 1) * dim, :] = state[:dim]
        sent_ref[h * dim : (h + 1) * dim, :] = state[:dim].astype(BF16)


def query_kernel(heads, normed_ref, w_ref, q_ref, gate_ref):
    for h in range(heads):
        u = normed_ref[h]
        q = jnp.dot(u, w_ref[h, :, :LANES], preferred_element_type=F32)
        q_ref[h] = jnp.maximum(q, 0.0).astype(BF16)
        gate_ref[h] = jax.nn.sigmoid(jnp.dot(u, w_ref[h, :, 3 * LANES :], preferred_element_type=F32))


def finish_kernel(heads, dim, taken, place_ref, mixed_ref, q_ref, gate_ref, state_ref, *refs):
    got_refs, out_ref = refs[:-1], refs[-1]
    place = place_ref[0]
    for h in range(heads):
        rows = slice(h * dim, (h + 1) * dim)
        state = state_ref[rows, :]
        for i, got_ref in enumerate(got_refs):
            state = state + jnp.where(taken(place, i), got_ref[rows, :].astype(F32), 0.0)
        state = jnp.concatenate([state, jnp.zeros((LANES - dim, LANES), F32)], axis=0)
        new = finish(mixed_ref[h].astype(F32), gate_ref[h], attend(q_ref[h], state), dim)
        out_ref[:, h * dim : (h + 1) * dim] = new[:, :dim]


def exchange_rounds(state, sent, axis):
    size = lax.axis_size(axis)
    paired = size & (size - 1) == 0
    got = []
    total = state
    step = 1
    while step < size:
        if paired:
            partners = [(i, i ^ step) for i in range(size)]
        else:
            partners = [(i, i + step) for i in range(size - step)]
        got.append(lax.ppermute(sent, axis, partners))
        step *= 2
        if step < size:
            total = total + got[-1].astype(F32)
            sent = total.astype(BF16)

    def taken(place, turn):
        return (place >> turn) & 1 == 1 if paired else place >= 1 << turn

    return got, taken


def body(latents, spatial_weights, causal_weights):
    frames, rows, cols, width = latents.shape
    maps, all_heads, dim, _ = spatial_weights.shape
    n_row = lax.axis_size("row")
    if frames != 1 or n_row != 2 or dim > LANES:
        raise ValueError("unsupported shapes")
    heads = all_heads // n_row
    band = frames * rows * cols
    tokens = n_row * band
    row = jnp.reshape(lax.axis_index("row"), (1,)).astype(jnp.int32)
    place = jnp.reshape(lax.axis_index("frame"), (1,)).astype(jnp.int32)
    swap = [(i, n_row - 1 - i) for i in range(n_row)]

    own = latents.reshape(band, width)
    other = lax.ppermute(own, "row", swap)

    packed = jax.ShapeDtypeStruct((heads, LANES, maps * LANES), BF16)
    ws, wc = call(
        functools.partial(pack_kernel, heads), "pack", [packed, packed],
        [row, spatial_weights, causal_weights], [SMEM, VMEM, VMEM],
    )

    head_bf16 = jax.ShapeDtypeStruct((heads, tokens, LANES), BF16)
    head_f32 = jax.ShapeDtypeStruct((heads, tokens, LANES), F32)
    token_f32 = jax.ShapeDtypeStruct((tokens, LANES), F32)
    mixed, part = call(
        functools.partial(spatial_kernel, heads, dim, n_row), "spatial", [head_bf16, token_f32],
        [row, own, other, ws], [SMEM, VMEM, VMEM, VMEM],
        [pltpu.VMEM((heads, tokens, LANES), BF16), pltpu.VMEM((tokens, LANES), F32)],
        flops=2 * tokens * heads * LANES * LANES * 6,
    )
    part_other = lax.ppermute(part, "row", swap)

    normed, state, sent = call(
        functools.partial(state_kernel, heads, dim, width), "state",
        [head_bf16, jax.ShapeDtypeStruct((heads * dim, LANES), F32), jax.ShapeDtypeStruct((heads * dim, LANES), BF16)],
        [mixed, part, part_other, wc], [VMEM] * 4,
        flops=2 * tokens * heads * LANES * LANES * 3,
    )
    got, taken = exchange_rounds(state, sent, "frame")
    q, gate = call(
        functools.partial(query_kernel, heads), "query", [head_bf16, head_f32],
        [normed, wc], [VMEM, VMEM],
        flops=2 * tokens * heads * LANES * LANES * 2,
    )
    (out,) = call(
        functools.partial(finish_kernel, heads, dim, taken), "finish",
        [jax.ShapeDtypeStruct((tokens, heads * dim), BF16)],
        [place, mixed, q, gate, state, *got], [SMEM] + [VMEM] * (4 + len(got)),
        flops=2 * tokens * heads * LANES * LANES,
    )
    return out.reshape(frames, n_row * rows, cols, heads * dim)


def solution(mesh):
    in_specs = (P(("group", "frame"), "row", None, None), P(), P())
    out_specs = P(("group", "frame"), None, None, "row")
    return jax.shard_map(body, mesh=mesh, in_specs=in_specs, out_specs=out_specs, check_vma=False)
```

time: 120 us -> 32.8 us (0.27)
  the two profiles are of different devices: /device:TPU:27 before, /device:TPU:0 now
where the time goes in v1:
time: 32.8 us; the launch traced here: 32.6 us
  waiting for transfers between devices  14.8 us (45%)
  starting transfers between devices  8 us (24%)
  Pallas kernels  6.41 us (20%)
  local copies, waits for them, and re-layouts  3.19 us (10%)
    ppermute x3, waiting for transfers between devices, exchange_rounds(): got.append(lax.ppermute(sent, axis, partners))  13.6 us
    ppermute x3, starting transfers between devices, exchange_rounds(): got.append(lax.ppermute(sent, axis, partners))  7.31 us
    pallas_call x5, Pallas kernels, call(): pl.pallas_call(kernel, name=name, out_shape=tuple(out_shape), in_specs=in...  6.41 us
    unnamed x6, local copies, waits for them, and re-layouts  3.19 us
    ppermute x1, waiting for transfers between devices, body(): part_other = lax.ppermute(part, 'row', swap)  1.22 us
  transfers between devices with their start and end apart: 5, of which 4 were waited for; matrix products, arithmetic and copies ran while one was open for 0% of the time, Pallas kernels for 2%

profile of v1, /device:TPU:0, one launch (start us, length us, event | category | flops | bytes accessed | tf_op | source)
XLA Modules:
  0.0 32.6 jit_solution(12217285337366628892)
XLA Ops:
  0.0 0.5 %collective-permute-start = (bf16[128,1120]{1,0:T(8,128)(2,1)}, bf16[128,1120]{1,0:T(8,128)(2,1)S(1)}, u32[]{:S(2)}, u32[]{:S(2)}) collective-permute-start(bf16[128,1120]{1,0:T(8,128)(2,1)} %bitcast.4), channel_id=1, source_target_pairs={{0,1},{1,0},{2,3},{3,2},{4,5},{5,4},{6,7},{7,6},{8,9},{9,8},{10,11... | collective-permute-start | bytes 860168 | tf_op jit(solution)/shard_map/ppermute | solution.py:165
  0.5 0.0 copy-start
  0.5 1.3 %copy-done = bf16[4,10,112,112]{3,2,1,0:T(8,128)(2,1)S(1)} copy-done((bf16[4,10,112,112]{3,2,1,0:T(8,128)(2,1)S(1)}, bf16[4,10,112,112]{3,2,1,0:T(8,128)(2,1)}, u32[]{:S(2)}) %copy-start) | copy-done | bytes 1003544
  1.8 0.0 copy-start.1
  1.8 1.3 %copy-done.1 = bf16[4,10,112,112]{3,2,1,0:T(8,128)(2,1)S(1)} copy-done((bf16[4,10,112,112]{3,2,1,0:T(8,128)(2,1)S(1)}, bf16[4,10,112,112]{3,2,1,0:T(8,128)(2,1)}, u32[]{:S(2)}) %copy-start.1) | copy-done | bytes 1003544
  3.0 0.0 copy-start.2
  3.0 0.3 pack.1
  3.3 0.0 collective-permute-done.other_ref
  3.3 0.7 %copy-done.2 = bf16[1,4,32,1120]{3,2,1,0:T(8,128)(2,1)S(1)} copy-done((bf16[1,4,32,1120]{3,2,1,0:T(8,128)(2,1)S(1)}, bf16[1,4,32,1120]{3,2,1,0:T(8,128)(2,1)}, u32[]{:S(2)}) %copy-start.2) | copy-done | bytes 286744
  4.0 2.8 %spatial.1 = (bf16[5,256,128]{2,1,0:T(8,128)(2,1)S(1)}, f32[256,128]{1,0:T(8,128)S(1)}) custom-call(s32[1]{0:T(128)} %bitcast.1.row_ref, bf16[128,1120]{1,0:T(8,128)(2,1)S(1)} %bitcast.5, bf16[128,1120]{1,0:T(8,128)(2,1)S(1)} %collective-permute-done.other_ref, bf16[5,128,512]{2,1,0:T(8,128)(2,1)S(1)} %get-tuple-element.14.w_ref), custom_call_target="tpu_custom_call" | custom-call | flops 251658240 | bytes 1687556 | tf_op jit(solution)/shard_map/spatial/pallas_call | solution.py:20
  6.7 0.2 collective-permute-start.1
  6.9 1.2 %collective-permute-done.1.part_other_ref = f32[256,128]{1,0:T(8,128)S(1)} collective-permute-done((f32[256,128]{1,0:T(8,128)S(1)}, f32[256,128]{1,0:T(8,128)S(1)}, u32[]{:S(2)}, u32[]{:S(2)}) %collective-permute-start.1) | collective-permute-done | bytes 131104 | tf_op jit(solution)/shard_map/ppermute | solution.py:182
  8.2 1.5 %state.1 = (bf16[5,256,128]{2,1,0:T(8,128)(2,1)S(1)}, f32[560,128]{1,0:T(8,128)S(1)}, bf16[560,128]{1,0:T(8,128)(2,1)S(1)}) custom-call(bf16[5,256,128]{2,1,0:T(8,128)(2,1)S(1)} %get-tuple-element.15.mixed_ref, f32[256,128]{1,0:T(8,128)S(1)} %get-tuple-element.16.part_ref, f32[256,128]{1,0:T(8,128)S(1)} %collective-permute-done.1.part_other_ref, ...), custom_call_target="tpu_custom_call" | custom-call | flops 125829120 | bytes 2002944 | tf_op jit(solution)/shard_map/state/pallas_call | solution.py:20
  9.6 2.8 %collective-permute-start.2 = (bf16[560,128]{1,0:T(8,128)(2,1)S(1)}, bf16[560,128]{1,0:T(8,128)(2,1)S(1)}, u32[]{:S(2)}, u32[]{:S(2)}) collective-permute-start(bf16[560,128]{1,0:T(8,128)(2,1)S(1)} %get-tuple-element.22), channel_id=1, source_target_pairs={{0,2},{2,0},{4,6},{6,4},{8,10},{10,8},{12,14},{14,12},{1,3},{3,1},... | collective-permute-start | bytes 430088 | tf_op jit(solution)/shard_map/ppermute | solution.py:139
  12.4 4.3 %collective-permute-done.2.refs_0_ = bf16[560,128]{1,0:T(8,128)(2,1)S(1)} collective-permute-done((bf16[560,128]{1,0:T(8,128)(2,1)S(1)}, bf16[560,128]{1,0:T(8,128)(2,1)S(1)}, u32[]{:S(2)}, u32[]{:S(2)}) %collective-permute-start.2) | collective-permute-done | bytes 143392 | tf_op jit(solution)/shard_map/ppermute | solution.py:139
  16.8 1.9 %collective-permute-start.3 = (bf16[560,128]{1,0:T(8,128)(2,1)S(1)}, bf16[560,128]{1,0:T(8,128)(2,1)S(1)}, u32[]{:S(2)}, u32[]{:S(2)}) collective-permute-start(bf16[560,128]{1,0:T(8,128)(2,1)S(1)} %fusion), channel_id=1, source_target_pairs={{0,4},{2,6},{4,0},{6,2},{8,12},{10,14},{12,8},{14,10},{1,5},{3,7},... | collective-permute-start | bytes 430088 | tf_op jit(solution)/shard_map/ppermute | solution.py:139
  18.7 3.6 %collective-permute-done.3.refs_1_ = bf16[560,128]{1,0:T(8,128)(2,1)S(1)} collective-permute-done((bf16[560,128]{1,0:T(8,128)(2,1)S(1)}, bf16[560,128]{1,0:T(8,128)(2,1)S(1)}, u32[]{:S(2)}, u32[]{:S(2)}) %collective-permute-start.3) | collective-permute-done | bytes 143392 | tf_op jit(solution)/shard_map/ppermute | solution.py:139
  22.3 0.1 add_convert_fusion
  22.4 2.6 %collective-permute-start.4 = (bf16[560,128]{1,0:T(8,128)(2,1)S(1)}, bf16[560,128]{1,0:T(8,128)(2,1)S(1)}, u32[]{:S(2)}, u32[]{:S(2)}) collective-permute-start(bf16[560,128]{1,0:T(8,128)(2,1)S(1)} %add_convert_fusion), channel_id=1, source_target_pairs={{0,8},{2,10},{4,12},{6,14},{8,0},{10,2},{12,4},{14,6},{1,9},{3,11}... | collective-permute-start | bytes 430088 | tf_op jit(solution)/shard_map/ppermute | solution.py:139
  25.0 0.3 query.1
  25.3 5.7 %collective-permute-done.4.refs_2_ = bf16[560,128]{1,0:T(8,128)(2,1)S(1)} collective-permute-done((bf16[560,128]{1,0:T(8,128)(2,1)S(1)}, bf16[560,128]{1,0:T(8,128)(2,1)S(1)}, u32[]{:S(2)}, u32[]{:S(2)}) %collective-permute-start.4) | collective-permute-done | bytes 143392 | tf_op jit(solution)/shard_map/ppermute | solution.py:139
  31.0 1.6 %finish.1 = bf16[256,560]{1,0:T(8,128)(2,1)} custom-call(s32[1]{0:T(128)} %bitcast.place_ref, bf16[5,256,128]{2,1,0:T(8,128)(2,1)S(1)} %get-tuple-element.15.mixed_ref, bf16[5,256,128]{2,1,0:T(8,128)(2,1)S(1)} %get-tuple-element.19.q_ref, f32[5,256,128]{2,1,0:T(8,128)S(1)} %get-tuple-element.20.gate_ref, f32[560,128]{1,0:T(8,128)S(1)} %get-tuple-element.21.state_ref, ...), custom_call_target="tpu_custom_call" | custom-call | flops 41943040 | bytes 2314244 | tf_op jit(solution)/shard_map/finish/pallas_call | solution.py:20
  (1 shorter events, 0.0 us)
Async XLA Ops:
  0.0 3.3 %collective-permute-start = (bf16[128,1120]{1,0:T(8,128)(2,1)}, bf16[128,1120]{1,0:T(8,128)(2,1)S(1)}, u32[]{:S(2)}, u32[]{:S(2)}) collective-permute-start(bf16[128,1120]{1,0:T(8,128)(2,1)} %bitcast.4), channel_id=1, source_target_pairs={{0,1},{1,0},{2,3},{3,2},{4,5},{5,4},{6,7},{7,6},{8,9},{9,8},{10,11... | collective-permute-start | bytes 860168 | tf_op jit(solution)/shard_map/ppermute | solution.py:165
  0.5 1.3 %copy-start = (bf16[4,10,112,112]{3,2,1,0:T(8,128)(2,1)S(1)}, bf16[4,10,112,112]{3,2,1,0:T(8,128)(2,1)}, u32[]{:S(2)}) copy-start(bf16[4,10,112,112]{3,2,1,0:T(8,128)(2,1)} %refs_0_.1) | copy-start | bytes 3010564
  1.8 1.3 %copy-start.1 = (bf16[4,10,112,112]{3,2,1,0:T(8,128)(2,1)S(1)}, bf16[4,10,112,112]{3,2,1,0:T(8,128)(2,1)}, u32[]{:S(2)}) copy-start(bf16[4,10,112,112]{3,2,1,0:T(8,128)(2,1)} %refs_1_.1) | copy-start | bytes 3010564
  3.0 1.0 %copy-start.2 = (bf16[1,4,32,1120]{3,2,1,0:T(8,128)(2,1)S(1)}, bf16[1,4,32,1120]{3,2,1,0:T(8,128)(2,1)}, u32[]{:S(2)}) copy-start(bf16[1,4,32,1120]{3,2,1,0:T(8,128)(2,1)} %param.3) | copy-start | bytes 860164
  6.7 1.4 %collective-permute-start.1 = (f32[256,128]{1,0:T(8,128)S(1)}, f32[256,128]{1,0:T(8,128)S(1)}, u32[]{:S(2)}, u32[]{:S(2)}) collective-permute-start(f32[256,128]{1,0:T(8,128)S(1)} %get-tuple-element.16.part_ref), channel_id=1, source_target_pairs={{0,1},{1,0},{2,3},{3,2},{4,5},{5,4},{6,7},{7,6},{8,9},{9,8},{10,11... | collective-permute-start | bytes 393224 | tf_op jit(solution)/shard_map/ppermute | solution.py:182
  9.6 7.1 %collective-permute-start.2 = (bf16[560,128]{1,0:T(8,128)(2,1)S(1)}, bf16[560,128]{1,0:T(8,128)(2,1)S(1)}, u32[]{:S(2)}, u32[]{:S(2)}) collective-permute-start(bf16[560,128]{1,0:T(8,128)(2,1)S(1)} %get-tuple-element.22), channel_id=1, source_target_pairs={{0,2},{2,0},{4,6},{6,4},{8,10},{10,8},{12,14},{14,12},{1,3},{3,1},... | collective-permute-start | bytes 430088 | tf_op jit(solution)/shard_map/ppermute | solution.py:139
  16.8 5.5 %collective-permute-start.3 = (bf16[560,128]{1,0:T(8,128)(2,1)S(1)}, bf16[560,128]{1,0:T(8,128)(2,1)S(1)}, u32[]{:S(2)}, u32[]{:S(2)}) collective-permute-start(bf16[560,128]{1,0:T(8,128)(2,1)S(1)} %fusion), channel_id=1, source_target_pairs={{0,4},{2,6},{4,0},{6,2},{8,12},{10,14},{12,8},{14,10},{1,5},{3,7},... | collective-permute-start | bytes 430088 | tf_op jit(solution)/shard_map/ppermute | solution.py:139
  22.4 8.6 %collective-permute-start.4 = (bf16[560,128]{1,0:T(8,128)(2,1)S(1)}, bf16[560,128]{1,0:T(8,128)(2,1)S(1)}, u32[]{:S(2)}, u32[]{:S(2)}) collective-permute-start(bf16[560,128]{1,0:T(8,128)(2,1)S(1)} %add_convert_fusion), channel_id=1, source_target_pairs={{0,8},{2,10},{4,12},{6,14},{8,0},{10,2},{12,4},{14,6},{1,9},{3,11}... | collective-permute-start | bytes 430088 | tf_op jit(solution)/shard_map/ppermute | solution.py:139

commit v2 on v1

v2 whole, which is shorter than its diff:
```python
import functools

import jax
import jax.numpy as jnp
from jax import lax
from jax.experimental import pallas as pl
from jax.experimental.pallas import tpu as pltpu
from jax.sharding import PartitionSpec as P

LANES = 128
SUBLANES = 8
F32 = jnp.float32
BF16 = jnp.bfloat16
VMEM = pl.BlockSpec(memory_space=pltpu.VMEM)
SMEM = pl.BlockSpec(memory_space=pltpu.SMEM)
HBM = pl.BlockSpec(memory_space=pltpu.HBM)


def call(kernel, name, outs, operands, in_specs, scratch=(), flops=0, limit=16 << 20, out_specs=None, aliases=None):
    n_bytes = sum(o.size * o.dtype.itemsize for o in operands)
    n_bytes += sum(o.size * o.dtype.itemsize for o in outs)
    return pl.pallas_call(
        kernel,
        name=name,
        out_shape=tuple(outs),
        in_specs=in_specs,
        out_specs=tuple(out_specs or [VMEM for _ in outs]),
        scratch_shapes=list(scratch),
        input_output_aliases=aliases or {},
        compiler_params=pltpu.CompilerParams(vmem_limit_bytes=limit),
        cost_estimate=pl.CostEstimate(flops=flops, bytes_accessed=n_bytes, transcendentals=0),
    )(*operands)


def fetch_maps(heads, row, w_hbm, w_ref, sems):
    first = row * heads
    copies = []
    for m in range(w_hbm.shape[0]):
        copies.append(pltpu.make_async_copy(w_hbm.at[m, pl.ds(first, heads)], w_ref.at[m], sems.at[m]))
        copies[-1].start()
    return copies


def pack_maps(heads, first, w_ref, out_ref, copies=()):
    dim = w_ref.shape[2]
    if dim < LANES:
        out_ref[:, dim:, :] = jnp.zeros((heads, LANES - dim, out_ref.shape[2]), BF16)
    for m in range(w_ref.shape[0]):
        if copies:
            copies[m].wait()
        for h in range(heads):
            block = w_ref[m, first + h]
            if dim < LANES:
                block = jnp.concatenate([block, jnp.zeros((dim, LANES - dim), BF16)], axis=1)
            out_ref[h, :dim, m * LANES : (m + 1) * LANES] = block


def split_heads(heads, dim, n_row, row, src_ref, u_ref, x_ref, at):
    band, width = src_ref.shape
    full = src_ref[...].astype(F32)
    inv = lax.rsqrt(jnp.sum(full * full, axis=-1, keepdims=True) / width + 1e-06)
    inv = jnp.broadcast_to(inv, (band, LANES))
    for r in range(n_row):

        @pl.when(row == r)
        def _():
            for h in range(heads):
                lo = (r * heads + h) * dim
                x = src_ref[:, lo : lo + dim]
                if dim < LANES:
                    x = jnp.concatenate([x, jnp.zeros((band, LANES - dim), BF16)], axis=1)
                x_ref[h, at, :] = x

    for h in range(heads):
        u_ref[h, at, :] = (x_ref[h, at, :].astype(F32) * inv).astype(BF16)


def lead_kernel(heads, dim, n_row, row_ref, own_hbm, w_hbm, u_ref, x_ref, maps_ref, own_ref, w_ref, sems):
    row = row_ref[0]
    mine = pltpu.make_async_copy(own_hbm, own_ref, sems.at[w_hbm.shape[0]])
    mine.start()
    copies = fetch_maps(heads, row, w_hbm, w_ref, sems)
    mine.wait()
    split_heads(heads, dim, n_row, row, own_ref, u_ref, x_ref, slice(None))
    pack_maps(heads, 0, w_ref, maps_ref, copies)


def pack_kernel(heads, row_ref, w_ref, maps_ref):
    pack_maps(heads, row_ref[0] * heads, w_ref, maps_ref)


def lane_blocks(sums, extra):
    blocks = sums.shape[0] // SUBLANES
    lane = lax.broadcasted_iota(jnp.int32, (SUBLANES, LANES), 1)
    tile = jnp.zeros((SUBLANES, LANES), F32)
    for b in range(blocks):
        here = lane == b
        if b < extra:
            here = jnp.logical_or(here, lane == blocks + b)
        tile = jnp.where(here, sums[b * SUBLANES : (b + 1) * SUBLANES, :], tile)
    return tile


def split_state(state):
    high = state.astype(BF16)
    low = (state - high.astype(F32)).astype(BF16)
    return jnp.concatenate([high, low], axis=0)


def attend(q, parts):
    return jnp.dot(jnp.concatenate([q, q], axis=1), parts, preferred_element_type=F32)


def finish(x, gate, attended, dim):
    inv_rms = lax.rsqrt(jnp.sum(attended * attended, axis=-1, keepdims=True) / dim + 1e-05)
    return (x + gate * attended * inv_rms).astype(BF16)


def outer_sum(k, v):
    return lax.dot_general(k, v, (((0,), (0,)), ((), ())), preferred_element_type=F32)


def spatial_kernel(
    heads, dim, n_row, row_ref, u_own_ref, x_own_ref, other_ref, w_ref,
    mixed_ref, part_ref, u_ref, x_ref, q_ref, k_ref, v_ref, gate_ref, parts_ref,
):
    band = other_ref.shape[0]
    split_heads(heads, dim, n_row, row_ref[0], other_ref, u_ref, x_ref, slice(None))
    for h in range(heads):
        u = jnp.concatenate([u_own_ref[h], u_ref[h]], axis=0)
        mapped = jnp.dot(u, w_ref[h], preferred_element_type=F32)
        q_ref[h] = jnp.maximum(mapped[:, :LANES], 0.0).astype(BF16)
        k_ref[h] = jnp.maximum(mapped[:, LANES : 2 * LANES], 0.0).astype(BF16)
        v_ref[h] = mapped[:, 2 * LANES : 3 * LANES].astype(BF16)
        gate_ref[h] = jax.nn.sigmoid(mapped[:, 3 * LANES :])
    for h in range(heads):
        parts_ref[h] = split_state(outer_sum(k_ref[h], v_ref[h]))
    part = jnp.zeros((2 * band, LANES), F32)
    for h in range(heads):
        x = jnp.concatenate([x_own_ref[h], x_ref[h]], axis=0).astype(F32)
        mixed = finish(x, gate_ref[h], attend(q_ref[h], parts_ref[h]), dim)
        mixed_ref[h] = mixed
        wide = mixed.astype(F32)
        part = part + wide * wide
    part_ref[...] = lane_blocks(jnp.sum(part, axis=-1, keepdims=True), band // SUBLANES)


def state_kernel(heads, dim, width, mixed_ref, part_ref, got_ref, w_ref, u_ref, parts_ref, sent_ref, k_ref, v_ref):
    blocks = mixed_ref.shape[1] // SUBLANES
    total = part_ref[...] + pltpu.roll(got_ref[...], LANES - blocks // 2, 1)
    tile = lax.rsqrt(total / width + 1e-06)
    inv = jnp.concatenate([jnp.broadcast_to(tile[:, b : b + 1], (SUBLANES, LANES)) for b in range(blocks)], axis=0)
    for h in range(heads):
        u = (mixed_ref[h].astype(F32) * inv).astype(BF16)
        u_ref[h] = u
        mapped = jnp.dot(u, w_ref[h, :, LANES : 3 * LANES], preferred_element_type=F32)
        k_ref[h] = jnp.maximum(mapped[:, :LANES], 0.0).astype(BF16)
        v_ref[h] = mapped[:, LANES:].astype(BF16)
    for h in range(heads):
        state = outer_sum(k_ref[h], v_ref[h])
        parts_ref[h] = split_state(state)
        store_packed(sent_ref, h, heads, dim, state[:dim].astype(BF16))


def packing(heads, dim):
    spare = LANES - dim
    if heads > 1 and spare and dim % spare == 0:
        for left in range(dim - 16, 0, -16):
            if (heads - 1) * (dim // left) >= dim // spare:
                return dim - left
    return dim


def packed_rows(heads, dim):
    return (heads - 1) * dim + packing(heads, dim)


def spare_blocks(heads, dim):
    kept = packing(heads, dim)
    left, spare = dim - kept, LANES - dim
    if not left:
        return []
    each = dim // left
    return [((c // each) * dim + (c % each) * left, c * spare) for c in range(dim // spare)]


def store_packed(ref, h, heads, dim, block):
    at = h * dim
    if h < heads - 1:
        ref[at : at + dim, :dim] = block[:, :dim]
        return
    kept = packing(heads, dim)
    ref[at : at + kept, :] = block[:kept]
    for row, lane in spare_blocks(heads, dim):
        ref[row : row + dim - kept, dim:] = block[kept:, lane : lane + LANES - dim]


def load_packed(ref, h, heads, dim, tail_ref):
    at = h * dim
    if h < heads - 1:
        block = ref[at : at + dim, :]
    else:
        kept = packing(heads, dim)
        tail_ref[:kept, :] = ref[at : at + kept, :]
        for row, lane in spare_blocks(heads, dim):
            tail_ref[kept:dim, lane : lane + LANES - dim] = ref[row : row + dim - kept, dim:]
        block = tail_ref[:dim, :]
    lane = lax.broadcasted_iota(jnp.int32, (dim, LANES), 1)
    block = jnp.where(lane < dim, block.astype(F32), 0.0)
    if dim < LANES:
        block = jnp.concatenate([block, jnp.zeros((LANES - dim, LANES), F32)], axis=0)
    return block


def write_out(heads, dim, n_row, row, mixed_ref, gate_ref, attended_ref, out_hbm, out_ref, sems):
    band = mixed_ref.shape[1] // n_row
    copies = []
    for b, place in enumerate((row, n_row - 1 - row)):
        at = slice(b * band, (b + 1) * band)
        for h in range(heads):
            new = finish(mixed_ref[h, at, :].astype(F32), gate_ref[h, at, :], attended_ref[h, at, :], dim)
            out_ref[at, h * dim : (h + 1) * dim] = new[:, :dim]
        to = pl.ds(pl.multiple_of(place * band, band), band)
        copies.append(pltpu.make_async_copy(out_ref.at[at], out_hbm.at[to], sems.at[b]))
        copies[-1].start()
    for copy in copies:
        copy.wait()


def query_kernel(heads, dim, n_row, taken, row_ref, place_ref, mixed_ref, u_ref, w_ref, parts_ref, *refs):
    got_refs, (q_ref, gate_ref, base_ref, out_hbm, out_ref, sum_ref, tail_ref, sems) = refs[:-8], refs[-8:]
    place = place_ref[0]
    if got_refs:
        earlier = jnp.zeros(sum_ref.shape, F32)
        for turn, got_ref in enumerate(got_refs):
            earlier = earlier + jnp.where(taken(place, turn), got_ref[...].astype(F32), 0.0)
        sum_ref[...] = earlier
    for h in range(heads):
        u = u_ref[h]
        q = jnp.maximum(jnp.dot(u, w_ref[h, :, :LANES], preferred_element_type=F32), 0.0).astype(BF16)
        q_ref[h] = q
        gate_ref[h] = jax.nn.sigmoid(jnp.dot(u, w_ref[h, :, 3 * LANES :], preferred_element_type=F32))
    for h in range(heads):
        base = attend(q_ref[h], parts_ref[h])
        if got_refs:
            base = base + attend(q_ref[h], split_state(load_packed(sum_ref, h, heads, dim, tail_ref)))
        base_ref[h] = base
    write_out(heads, dim, n_row, row_ref[0], mixed_ref, gate_ref, base_ref, out_hbm, out_ref, sems)


def finish_kernel(
    heads, dim, n_row, taken, turn, row_ref, place_ref, mixed_ref, q_ref, gate_ref, base_ref, got_ref, first_hbm,
    out_hbm, out_ref, state_ref, tail_ref, attended_ref, sems,
):
    @pl.when(taken(place_ref[0], turn))
    def _():
        for h in range(heads):
            state_ref[h] = load_packed(got_ref, h, heads, dim, tail_ref).astype(BF16)
        for h in range(heads):
            attended_ref[h] = base_ref[h] + jnp.dot(q_ref[h], state_ref[h], preferred_element_type=F32)
        write_out(heads, dim, n_row, row_ref[0], mixed_ref, gate_ref, attended_ref, out_hbm, out_ref, sems)


def exchange_rounds(sent, axis):
    size = lax.axis_size(axis)
    paired = size & (size - 1) == 0
    got = []
    total = sent.astype(F32)
    step = 1
    while step < size:
        if paired:
            partners = [(i, i ^ step) for i in range(size)]
        else:
            partners = [(i, i + step) for i in range(size - step)]
        got.append(lax.ppermute(sent, axis, partners))
        step *= 2
        if step < size:
            total = total + got[-1].astype(F32)
            sent = total.astype(BF16)

    def taken(place, turn):
        return (place >> turn) & 1 == 1 if paired else place >= 1 << turn

    return got, taken


def body(latents, spatial_weights, causal_weights):
    frames, rows, cols, width = latents.shape
    maps, all_heads, dim, _ = spatial_weights.shape
    n_row = lax.axis_size("row")
    if frames != 1 or n_row != 2 or dim > LANES or 3 * rows * cols > SUBLANES * LANES or lax.axis_size("frame") < 2:
        raise ValueError("unsupported shapes")
    heads = all_heads // n_row
    band = rows * cols
    tokens = n_row * band
    row = jnp.reshape(lax.axis_index("row"), (1,)).astype(jnp.int32)
    place = jnp.reshape(lax.axis_index("frame"), (1,)).astype(jnp.int32)
    swap = [(i, n_row - 1 - i) for i in range(n_row)]

    def shape(*dims, kind=BF16):
        return jax.ShapeDtypeStruct(dims, kind)

    packed_maps = shape(heads, LANES, maps * LANES)
    fetched = pltpu.VMEM((maps, heads, dim, dim), BF16)
    per_head = pltpu.VMEM((heads, tokens, LANES), BF16)
    band_head = pltpu.VMEM((heads, band, LANES), BF16)
    gates = pltpu.VMEM((heads, tokens, LANES), F32)

    own = latents.reshape(band, width)
    own_hbm = pltpu.with_memory_space_constraint(own, pltpu.HBM)
    spatial_weights = pltpu.with_memory_space_constraint(spatial_weights, pltpu.HBM)
    other = lax.ppermute(own, "row", swap)
    u_own, x_own, maps_s = call(
        functools.partial(lead_kernel, heads, dim, n_row), "lead",
        [shape(heads, band, LANES), shape(heads, band, LANES), packed_maps],
        [row, own_hbm, spatial_weights], [SMEM, HBM, HBM],
        [pltpu.VMEM((band, width), BF16), fetched, pltpu.SemaphoreType.DMA((maps + 1,))],
    )
    mixed, part = call(
        functools.partial(spatial_kernel, heads, dim, n_row), "spatial",
        [shape(heads, tokens, LANES), shape(SUBLANES, LANES, kind=F32)],
        [row, u_own, x_own, other, maps_s], [SMEM] + [VMEM] * 4,
        [band_head, band_head, per_head, per_head, per_head, gates, pltpu.VMEM((heads, 2 * LANES, LANES), BF16)],
        flops=2 * tokens * heads * LANES * LANES * 6,
    )
    causal_weights, part = lax.optimization_barrier((causal_weights, part))
    got_part = lax.ppermute(part, "row", swap)
    (maps_c,) = call(
        functools.partial(pack_kernel, heads), "pack", [packed_maps], [row, causal_weights], [SMEM, VMEM],
    )
    u, parts, sent = call(
        functools.partial(state_kernel, heads, dim, width), "state",
        [shape(heads, tokens, LANES), shape(heads, 2 * LANES, LANES), shape(packed_rows(heads, dim), LANES)],
        [mixed, part, got_part, maps_c], [VMEM] * 4, [per_head, per_head],
        flops=2 * tokens * heads * LANES * LANES * 3,
    )
    got, taken = exchange_rounds(sent, "frame")
    packed_sum = pltpu.VMEM((packed_rows(heads, dim), LANES), F32)
    whole = shape(tokens, heads * dim)
    writing = [pltpu.VMEM((tokens, heads * dim), BF16)]
    done = [pltpu.SemaphoreType.DMA((n_row,))]
    q, gate, base, out = call(
        functools.partial(query_kernel, heads, dim, n_row, taken), "query",
        [shape(heads, tokens, LANES), shape(heads, tokens, LANES, kind=F32), shape(heads, tokens, LANES, kind=F32), whole],
        [row, place, mixed, u, maps_c, parts, *got[:-1]], [SMEM] * 2 + [VMEM] * (3 + len(got)),
        writing + [packed_sum, pltpu.VMEM((LANES, LANES), F32)] + done,
        flops=2 * tokens * heads * LANES * LANES * 4, out_specs=[VMEM] * 3 + [HBM],
    )
    (out,) = call(
        functools.partial(finish_kernel, heads, dim, n_row, taken, len(got) - 1), "finish", [whole],
        [row, place, mixed, q, gate, base, got[-1], out], [SMEM] * 2 + [VMEM] * 5 + [HBM],
        writing + [pltpu.VMEM((heads, LANES, LANES), BF16), pltpu.VMEM((LANES, LANES), BF16), gates] + done,
        flops=2 * tokens * heads * LANES * LANES, out_specs=[HBM], aliases={7: 0},
    )
    return out.reshape(frames, n_row * rows, cols, heads * dim)


def solution(mesh):
    in_specs = (P(("group", "frame"), "row", None, None), P(), P())
    out_specs = P(("group", "frame"), None, None, "row")
    return jax.shard_map(body, mesh=mesh, in_specs=in_specs, out_specs=out_specs, check_vma=False)
```

time: 32.8 us -> 25.8 us (0.79)
  waiting for transfers between devices: 14.8 us -> 10.7 us
  local copies, waits for them, and re-layouts: 3.19 us -> 0.01 us
  starting transfers between devices: 8 us -> 8.43 us
    ppermute x3, waiting for transfers between devices: 13.6 us -> 10 us  [exchange_rounds(): got.append(lax.ppermute(sent, axis, partners))]
    unnamed x6 -> x2, local copies, waits for them, and re-layouts: 3.19 us -> 0.01 us
    ppermute x1, waiting for transfers between devices: 1.22 us -> 0.74 us  [body(): got_part = lax.ppermute(part, 'row', swap)]
    pallas_call x5 -> x6, Pallas kernels: 6.41 us -> 6.29 us  [call(): pl.pallas_call(kernel, name=name, out_shape=tuple(outs), in_specs=in_spec...]
  transfers between devices with their start and end apart: 5 -> 5, of which waited for: 4 -> 4; matrix products, arithmetic and copies ran while one was open for 0% -> 0% of each run, Pallas kernels for 2% -> 15%
where the time goes in v2:
time: 25.8 us; the launch traced here: 25.6 us
  waiting for transfers between devices  10.7 us (41%)
  starting transfers between devices  8.43 us (33%)
  Pallas kernels  6.29 us (24%)
    ppermute x3, waiting for transfers between devices, exchange_rounds(): got.append(lax.ppermute(sent, axis, partners))  10 us
    ppermute x3, starting transfers between devices, exchange_rounds(): got.append(lax.ppermute(sent, axis, partners))  7.5 us
    pallas_call x6, Pallas kernels, call(): pl.pallas_call(kernel, name=name, out_shape=tuple(outs), in_specs=in_spec...  6.29 us
    ppermute x1, waiting for transfers between devices, body(): got_part = lax.ppermute(part, 'row', swap)  0.74 us
  transfers between devices with their start and end apart: 5, of which 4 were waited for; matrix products, arithmetic and copies ran while one was open for 0% of the time, Pallas kernels for 15%

profile of v2, /device:TPU:0, one launch (start us, length us, event | category | flops | bytes accessed | tf_op | source)
XLA Modules:
  0.0 25.6 jit_solution(1546752500853945344)
XLA Ops:
  0.0 0.5 %collective-permute-start = (bf16[128,1120]{1,0:T(8,128)(2,1)}, bf16[128,1120]{1,0:T(8,128)(2,1)S(1)}, u32[]{:S(2)}, u32[]{:S(2)}) collective-permute-start(bf16[128,1120]{1,0:T(8,128)(2,1)} %bitcast.4), channel_id=1, source_target_pairs={{0,1},{1,0},{2,3},{3,2},{4,5},{5,4},{6,7},{7,6},{8,9},{9,8},{10,11... | collective-permute-start | bytes 860168 | tf_op jit(solution)/shard_map/ppermute | solution.py:312
  0.5 0.0 copy-start
  0.5 1.4 %lead.1 = (bf16[5,128,128]{2,1,0:T(8,128)(2,1)S(1)}, bf16[5,128,128]{2,1,0:T(8,128)(2,1)S(1)}, bf16[5,128,512]{2,1,0:T(8,128)(2,1)S(1)}) custom-call(s32[1]{0:T(128)} %bitcast.row_ref, bf16[128,1120]{1,0:T(8,128)(2,1)} %bitcast.5, bf16[4,10,112,112]{3,2,1,0:T(8,128)(2,1)} %w_hbm.1), custom_call_target="tpu_custom_call" | custom-call | bytes 2273284 | tf_op jit(solution)/shard_map/lead/pallas_call | solution.py:22
  1.9 0.0 collective-permute-done.other_ref
  2.0 1.5 %spatial.1 = (bf16[5,256,128]{2,1,0:T(8,128)(2,1)S(1)}, f32[8,128]{1,0:T(8,128)S(1)}) custom-call(s32[1]{0:T(128)} %bitcast.row_ref, bf16[5,128,128]{2,1,0:T(8,128)(2,1)S(1)} %get-tuple-element.19.u_own_ref, bf16[5,128,128]{2,1,0:T(8,128)(2,1)S(1)} %get-tuple-element.20.x_own_ref, bf16[128,1120]{1,0:T(8,128)(2,1)S(1)} %collective-permute-done.other_ref, ...), custom_call_target="tpu_custom_call" | custom-call | flops 251658240 | bytes 1601540 | tf_op jit(solution)/shard_map/spatial/pallas_call | solution.py:22
  3.5 0.4 %collective-permute-start.1 = (f32[8,128]{1,0:T(8,128)S(1)}, f32[8,128]{1,0:T(8,128)S(1)}, u32[]{:S(2)}, u32[]{:S(2)}) collective-permute-start(f32[8,128]{1,0:T(8,128)S(1)} %get-tuple-element.24.part_ref), channel_id=1, source_target_pairs={{0,1},{1,0},{2,3},{3,2},{4,5},{5,4},{6,7},{7,6},{8,9},{9,8},{10,11... | collective-permute-start | bytes 12296 | tf_op jit(solution)/shard_map/ppermute | solution.py:327
  3.9 0.0 copy-done
  3.9 0.1 pack.1.w_ref
  4.0 0.7 %collective-permute-done.1.got_ref = f32[8,128]{1,0:T(8,128)S(1)} collective-permute-done((f32[8,128]{1,0:T(8,128)S(1)}, f32[8,128]{1,0:T(8,128)S(1)}, u32[]{:S(2)}, u32[]{:S(2)}) %collective-permute-start.1) | collective-permute-done | bytes 4128 | tf_op jit(solution)/shard_map/ppermute | solution.py:327
  4.7 0.8 %state.1 = (bf16[5,256,128]{2,1,0:T(8,128)(2,1)S(1)}, bf16[5,256,128]{2,1,0:T(8,128)(2,1)S(1)}, bf16[512,128]{1,0:T(8,128)(2,1)S(1)}) custom-call(bf16[5,256,128]{2,1,0:T(8,128)(2,1)S(1)} %get-tuple-element.22.mixed_ref, f32[8,128]{1,0:T(8,128)S(1)} %get-tuple-element.24.part_ref, f32[8,128]{1,0:T(8,128)S(1)} %collective-permute-done.1.got_ref, ...), custom_call_target="tpu_custom_call" | custom-call | flops 125829120 | bytes 1777664 | tf_op jit(solution)/shard_map/state/pallas_call | solution.py:22
  5.5 2.8 %collective-permute-start.2 = (bf16[512,128]{1,0:T(8,128)(2,1)S(1)}, bf16[512,128]{1,0:T(8,128)(2,1)S(1)}, u32[]{:S(2)}, u32[]{:S(2)}) collective-permute-start(bf16[512,128]{1,0:T(8,128)(2,1)S(1)} %get-tuple-element.28), channel_id=1, source_target_pairs={{0,2},{2,0},{4,6},{6,4},{8,10},{10,8},{12,14},{14,12},{1,3},{3,1},... | collective-permute-start | bytes 393224 | tf_op jit(solution)/shard_map/ppermute | solution.py:275
  8.4 3.9 %collective-permute-done.2.refs_0_ = bf16[512,128]{1,0:T(8,128)(2,1)S(1)} collective-permute-done((bf16[512,128]{1,0:T(8,128)(2,1)S(1)}, bf16[512,128]{1,0:T(8,128)(2,1)S(1)}, u32[]{:S(2)}, u32[]{:S(2)}) %collective-permute-start.2) | collective-permute-done | bytes 131104 | tf_op jit(solution)/shard_map/ppermute | solution.py:275
  12.4 1.9 %collective-permute-start.3 = (bf16[512,128]{1,0:T(8,128)(2,1)S(1)}, bf16[512,128]{1,0:T(8,128)(2,1)S(1)}, u32[]{:S(2)}, u32[]{:S(2)}) collective-permute-start(bf16[512,128]{1,0:T(8,128)(2,1)S(1)} %fusion), channel_id=1, source_target_pairs={{0,4},{2,6},{4,0},{6,2},{8,12},{10,14},{12,8},{14,10},{1,5},{3,7},... | collective-permute-start | bytes 393224 | tf_op jit(solution)/shard_map/ppermute | solution.py:275
  14.2 3.3 %collective-permute-done.3.refs_1_ = bf16[512,128]{1,0:T(8,128)(2,1)S(1)} collective-permute-done((bf16[512,128]{1,0:T(8,128)(2,1)S(1)}, bf16[512,128]{1,0:T(8,128)(2,1)S(1)}, u32[]{:S(2)}, u32[]{:S(2)}) %collective-permute-start.3) | collective-permute-done | bytes 131104 | tf_op jit(solution)/shard_map/ppermute | solution.py:275
  17.5 0.1 add_convert_fusion
  17.6 2.8 %collective-permute-start.4 = (bf16[512,128]{1,0:T(8,128)(2,1)S(1)}, bf16[512,128]{1,0:T(8,128)(2,1)S(1)}, u32[]{:S(2)}, u32[]{:S(2)}) collective-permute-start(bf16[512,128]{1,0:T(8,128)(2,1)S(1)} %add_convert_fusion), channel_id=1, source_target_pairs={{0,8},{2,10},{4,12},{6,14},{8,0},{10,2},{12,4},{14,6},{1,9},{3,11}... | collective-permute-start | bytes 393224 | tf_op jit(solution)/shard_map/ppermute | solution.py:275
  20.3 2.4 %query.1 = (bf16[5,256,128]{2,1,0:T(8,128)(2,1)S(1)}, f32[5,256,128]{2,1,0:T(8,128)S(1)}, f32[5,256,128]{2,1,0:T(8,128)S(1)}, bf16[256,560]{1,0:T(8,128)(2,1)}) custom-call(s32[1]{0:T(128)} %bitcast.row_ref, s32[1]{0:T(128)} %bitcast.1.place_ref, bf16[5,256,128]{2,1,0:T(8,128)(2,1)S(1)} %get-tuple-element.22.mixed_ref, ...), custom_call_target="tpu_custom_call" | custom-call | flops 167772160 | bytes 3825672 | tf_op jit(solution)/shard_map/query/pallas_call | solution.py:22
  22.8 2.8 %collective-permute-done.4.got_ref = bf16[512,128]{1,0:T(8,128)(2,1)S(1)} collective-permute-done((bf16[512,128]{1,0:T(8,128)(2,1)S(1)}, bf16[512,128]{1,0:T(8,128)(2,1)S(1)}, u32[]{:S(2)}, u32[]{:S(2)}) %collective-permute-start.4) | collective-permute-done | bytes 131104 | tf_op jit(solution)/shard_map/ppermute | solution.py:275
  (2 shorter events, 0.1 us)
Async XLA Ops:
  0.0 1.9 %collective-permute-start = (bf16[128,1120]{1,0:T(8,128)(2,1)}, bf16[128,1120]{1,0:T(8,128)(2,1)S(1)}, u32[]{:S(2)}, u32[]{:S(2)}) collective-permute-start(bf16[128,1120]{1,0:T(8,128)(2,1)} %bitcast.4), channel_id=1, source_target_pairs={{0,1},{1,0},{2,3},{3,2},{4,5},{5,4},{6,7},{7,6},{8,9},{9,8},{10,11... | collective-permute-start | bytes 860168 | tf_op jit(solution)/shard_map/ppermute | solution.py:312
  0.5 3.4 %copy-start = (bf16[4,10,112,112]{3,2,1,0:T(8,128)(2,1)S(1)}, bf16[4,10,112,112]{3,2,1,0:T(8,128)(2,1)}, u32[]{:S(2)}) copy-start(bf16[4,10,112,112]{3,2,1,0:T(8,128)(2,1)} %w_ref) | copy-start | bytes 3010564
  3.5 1.3 %collective-permute-start.1 = (f32[8,128]{1,0:T(8,128)S(1)}, f32[8,128]{1,0:T(8,128)S(1)}, u32[]{:S(2)}, u32[]{:S(2)}) collective-permute-start(f32[8,128]{1,0:T(8,128)S(1)} %get-tuple-element.24.part_ref), channel_id=1, source_target_pairs={{0,1},{1,0},{2,3},{3,2},{4,5},{5,4},{6,7},{7,6},{8,9},{9,8},{10,11... | collective-permute-start | bytes 12296 | tf_op jit(solution)/shard_map/ppermute | solution.py:327
  5.5 6.8 %collective-permute-start.2 = (bf16[512,128]{1,0:T(8,128)(2,1)S(1)}, bf16[512,128]{1,0:T(8,128)(2,1)S(1)}, u32[]{:S(2)}, u32[]{:S(2)}) collective-permute-start(bf16[512,128]{1,0:T(8,128)(2,1)S(1)} %get-tuple-element.28), channel_id=1, source_target_pairs={{0,2},{2,0},{4,6},{6,4},{8,10},{10,8},{12,14},{14,12},{1,3},{3,1},... | collective-permute-start | bytes 393224 | tf_op jit(solution)/shard_map/ppermute | solution.py:275
  12.4 5.2 %collective-permute-start.3 = (bf16[512,128]{1,0:T(8,128)(2,1)S(1)}, bf16[512,128]{1,0:T(8,128)(2,1)S(1)}, u32[]{:S(2)}, u32[]{:S(2)}) collective-permute-start(bf16[512,128]{1,0:T(8,128)(2,1)S(1)} %fusion), channel_id=1, source_target_pairs={{0,4},{2,6},{4,0},{6,2},{8,12},{10,14},{12,8},{14,10},{1,5},{3,7},... | collective-permute-start | bytes 393224 | tf_op jit(solution)/shard_map/ppermute | solution.py:275
  17.6 8.0 %collective-permute-start.4 = (bf16[512,128]{1,0:T(8,128)(2,1)S(1)}, bf16[512,128]{1,0:T(8,128)(2,1)S(1)}, u32[]{:S(2)}, u32[]{:S(2)}) collective-permute-start(bf16[512,128]{1,0:T(8,128)(2,1)S(1)} %add_convert_fusion), channel_id=1, source_target_pairs={{0,8},{2,10},{4,12},{6,14},{8,0},{10,2},{12,4},{14,6},{1,9},{3,11}... | collective-permute-start | bytes 393224 | tf_op jit(solution)/shard_map/ppermute | solution.py:275

commit v3 on v2

--- a/solution.py
+++ b/solution.py
@@ -214,14 +214,13 @@
 
 def write_out(heads, dim, n_row, row, mixed_ref, gate_ref, attended_ref, out_hbm, out_ref, sems):
     band = mixed_ref.shape[1] // n_row
+    for h in range(heads):
+        new = finish(mixed_ref[h].astype(F32), gate_ref[h], attended_ref[h], dim)
+        out_ref[:, h * dim : (h + 1) * dim] = new[:, :dim]
     copies = []
     for b, place in enumerate((row, n_row - 1 - row)):
-        at = slice(b * band, (b + 1) * band)
-        for h in range(heads):
-            new = finish(mixed_ref[h, at, :].astype(F32), gate_ref[h, at, :], attended_ref[h, at, :], dim)
-            out_ref[at, h * dim : (h + 1) * dim] = new[:, :dim]
         to = pl.ds(pl.multiple_of(place * band, band), band)
-        copies.append(pltpu.make_async_copy(out_ref.at[at], out_hbm.at[to], sems.at[b]))
+        copies.append(pltpu.make_async_copy(out_ref.at[b * band : (b + 1) * band], out_hbm.at[to], sems.at[b]))
         copies[-1].start()
     for copy in copies:
         copy.wait()
@@ -263,23 +262,27 @@
 
 def exchange_rounds(sent, axis):
     size = lax.axis_size(axis)
-    paired = size & (size - 1) == 0
-    got = []
+    if size & (size - 1):
+        raise ValueError("unsupported mesh")
+    got, masks = [], []
     total = sent.astype(F32)
-    step = 1
-    while step < size:
-        if paired:
-            partners = [(i, i ^ step) for i in range(size)]
+    block = 1
+    while block < size:
+        if 4 * block <= size:
+            turn = [3 * block, 2 * block, block]
         else:
-            partners = [(i, i + step) for i in range(size - step)]
-        got.append(lax.ppermute(sent, axis, partners))
-        step *= 2
-        if step < size:
-            total = total + got[-1].astype(F32)
+            turn = [block + block // 2]
+        arrived = [lax.ppermute(sent, axis, [(i, i ^ mask) for i in range(size)]) for mask in turn]
+        got += arrived
+        masks += turn
+        block *= len(turn) + 1
+        if block < size:
+            for one in arrived:
+                total = total + one.astype(F32)
             sent = total.astype(BF16)
 
     def taken(place, turn):
-        return (place >> turn) & 1 == 1 if paired else place >= 1 << turn
+        return (place >> (masks[turn].bit_length() - 1)) & 1 == 1
 
     return got, taken
 

time: 25.8 us -> 24.6 us (0.953)
  the two profiles are of different devices: /device:TPU:0 before, /device:TPU:20 now
where the time goes in v3:
time: 24.6 us; the launch traced here: 24.4 us
  waiting for transfers between devices  12.1 us (49%)
  Pallas kernels  7.81 us (32%)
  starting transfers between devices  4.41 us (18%)
    ppermute x4, waiting for transfers between devices, exchange_rounds(): lax.ppermute(sent, axis, [(i, i ^ mask) for i in range(size)])  11 us
    pallas_call x6, Pallas kernels, call(): pl.pallas_call(kernel, name=name, out_shape=tuple(outs), in_specs=in_spec...  7.81 us
    ppermute x4, starting transfers between devices, exchange_rounds(): lax.ppermute(sent, axis, [(i, i ^ mask) for i in range(size)])  4.07 us
    ppermute x1, waiting for transfers between devices, body(): got_part = lax.ppermute(part, 'row', swap)  0.81 us
  transfers between devices with their start and end apart: 6, of which 6 were waited for; matrix products, arithmetic and copies ran while one was open for 0% of the time, Pallas kernels for 17%

profile of v3, /device:TPU:20, one launch (start us, length us, event | category | flops | bytes accessed | tf_op | source)
XLA Modules:
  0.0 24.4 jit_solution(7646872702948581570)
XLA Ops:
  0.0 0.0 collective-permute-start
  0.0 0.0 copy-start
  0.0 1.4 %lead.1 = (bf16[5,128,128]{2,1,0:T(8,128)(2,1)S(1)}, bf16[5,128,128]{2,1,0:T(8,128)(2,1)S(1)}, bf16[5,128,512]{2,1,0:T(8,128)(2,1)S(1)}) custom-call(s32[1]{0:T(128)} %bitcast.row_ref, bf16[128,1120]{1,0:T(8,128)(2,1)} %bitcast.5, bf16[4,10,112,112]{3,2,1,0:T(8,128)(2,1)} %w_hbm.1), custom_call_target="tpu_custom_call" | custom-call | bytes 2273284 | tf_op jit(solution)/shard_map/lead/pallas_call | solution.py:22
  1.5 0.3 %collective-permute-done.other_ref = bf16[128,1120]{1,0:T(8,128)(2,1)S(1)} collective-permute-done((bf16[128,1120]{1,0:T(8,128)(2,1)}, bf16[128,1120]{1,0:T(8,128)(2,1)S(1)}, u32[]{:S(2)}, u32[]{:S(2)}) %collective-permute-start) | collective-permute-done | bytes 286752 | tf_op jit(solution)/shard_map/ppermute | solution.py:315
  1.8 1.5 %spatial.1 = (bf16[5,256,128]{2,1,0:T(8,128)(2,1)S(1)}, f32[8,128]{1,0:T(8,128)S(1)}) custom-call(s32[1]{0:T(128)} %bitcast.row_ref, bf16[5,128,128]{2,1,0:T(8,128)(2,1)S(1)} %get-tuple-element.19.u_own_ref, bf16[5,128,128]{2,1,0:T(8,128)(2,1)S(1)} %get-tuple-element.20.x_own_ref, bf16[128,1120]{1,0:T(8,128)(2,1)S(1)} %collective-permute-done.other_ref, ...), custom_call_target="tpu_custom_call" | custom-call | flops 251658240 | bytes 1601540 | tf_op jit(solution)/shard_map/spatial/pallas_call | solution.py:22
  3.3 0.3 %collective-permute-start.1 = (f32[8,128]{1,0:T(8,128)S(1)}, f32[8,128]{1,0:T(8,128)S(1)}, u32[]{:S(2)}, u32[]{:S(2)}) collective-permute-start(f32[8,128]{1,0:T(8,128)S(1)} %get-tuple-element.24.part_ref), channel_id=1, source_target_pairs={{0,1},{1,0},{2,3},{3,2},{4,5},{5,4},{6,7},{7,6},{8,9},{9,8},{10,11... | collective-permute-start | bytes 12296 | tf_op jit(solution)/shard_map/ppermute | solution.py:330
  3.6 0.0 copy-done
  3.6 0.1 pack.1.w_ref
  3.7 0.8 %collective-permute-done.1.got_ref = f32[8,128]{1,0:T(8,128)S(1)} collective-permute-done((f32[8,128]{1,0:T(8,128)S(1)}, f32[8,128]{1,0:T(8,128)S(1)}, u32[]{:S(2)}, u32[]{:S(2)}) %collective-permute-start.1) | collective-permute-done | bytes 4128 | tf_op jit(solution)/shard_map/ppermute | solution.py:330
  4.5 0.8 %state.1 = (bf16[5,256,128]{2,1,0:T(8,128)(2,1)S(1)}, bf16[5,256,128]{2,1,0:T(8,128)(2,1)S(1)}, bf16[512,128]{1,0:T(8,128)(2,1)S(1)}) custom-call(bf16[5,256,128]{2,1,0:T(8,128)(2,1)S(1)} %get-tuple-element.22.mixed_ref, f32[8,128]{1,0:T(8,128)S(1)} %get-tuple-element.24.part_ref, f32[8,128]{1,0:T(8,128)S(1)} %collective-permute-done.1.got_ref, ...), custom_call_target="tpu_custom_call" | custom-call | flops 125829120 | bytes 1777664 | tf_op jit(solution)/shard_map/state/pallas_call | solution.py:22
  5.3 1.6 %collective-permute-start.4 = (bf16[512,128]{1,0:T(8,128)(2,1)S(1)}, bf16[512,128]{1,0:T(8,128)(2,1)S(1)}, u32[]{:S(2)}, u32[]{:S(2)}) collective-permute-start(bf16[512,128]{1,0:T(8,128)(2,1)S(1)} %get-tuple-element.28), channel_id=1, source_target_pairs={{0,2},{2,0},{4,6},{6,4},{8,10},{10,8},{12,14},{14,12},{1,3},{3,1},... | collective-permute-start | bytes 393224 | tf_op jit(solution)/shard_map/ppermute | solution.py:275
  6.9 1.6 %collective-permute-start.3 = (bf16[512,128]{1,0:T(8,128)(2,1)S(1)}, bf16[512,128]{1,0:T(8,128)(2,1)S(1)}, u32[]{:S(2)}, u32[]{:S(2)}) collective-permute-start(bf16[512,128]{1,0:T(8,128)(2,1)S(1)} %get-tuple-element.28), channel_id=1, source_target_pairs={{0,4},{2,6},{4,0},{6,2},{8,12},{10,14},{12,8},{14,10},{1,5},{3,7},... | collective-permute-start | bytes 393224 | tf_op jit(solution)/shard_map/ppermute | solution.py:275
  8.5 0.4 %collective-permute-start.2 = (bf16[512,128]{1,0:T(8,128)(2,1)S(1)}, bf16[512,128]{1,0:T(8,128)(2,1)S(1)}, u32[]{:S(2)}, u32[]{:S(2)}) collective-permute-start(bf16[512,128]{1,0:T(8,128)(2,1)S(1)} %get-tuple-element.28), channel_id=1, source_target_pairs={{0,6},{2,4},{4,2},{6,0},{8,14},{10,12},{12,10},{14,8},{1,7},{3,5},... | collective-permute-start | bytes 393224 | tf_op jit(solution)/shard_map/ppermute | solution.py:275
  8.9 2.2 %collective-permute-done.4.refs_2_ = bf16[512,128]{1,0:T(8,128)(2,1)S(1)} collective-permute-done((bf16[512,128]{1,0:T(8,128)(2,1)S(1)}, bf16[512,128]{1,0:T(8,128)(2,1)S(1)}, u32[]{:S(2)}, u32[]{:S(2)}) %collective-permute-start.4) | collective-permute-done | bytes 131104 | tf_op jit(solution)/shard_map/ppermute | solution.py:275
  11.1 2.2 %collective-permute-done.3.refs_1_ = bf16[512,128]{1,0:T(8,128)(2,1)S(1)} collective-permute-done((bf16[512,128]{1,0:T(8,128)(2,1)S(1)}, bf16[512,128]{1,0:T(8,128)(2,1)S(1)}, u32[]{:S(2)}, u32[]{:S(2)}) %collective-permute-start.3) | collective-permute-done | bytes 131104 | tf_op jit(solution)/shard_map/ppermute | solution.py:275
  13.3 1.8 %collective-permute-done.2.refs_0_ = bf16[512,128]{1,0:T(8,128)(2,1)S(1)} collective-permute-done((bf16[512,128]{1,0:T(8,128)(2,1)S(1)}, bf16[512,128]{1,0:T(8,128)(2,1)S(1)}, u32[]{:S(2)}, u32[]{:S(2)}) %collective-permute-start.2) | collective-permute-done | bytes 131104 | tf_op jit(solution)/shard_map/ppermute | solution.py:275
  15.1 0.1 add_convert_fusion
  15.1 0.5 %collective-permute-start.5 = (bf16[512,128]{1,0:T(8,128)(2,1)S(1)}, bf16[512,128]{1,0:T(8,128)(2,1)S(1)}, u32[]{:S(2)}, u32[]{:S(2)}) collective-permute-start(bf16[512,128]{1,0:T(8,128)(2,1)S(1)} %add_convert_fusion), channel_id=1, source_target_pairs={{0,12},{2,14},{4,8},{6,10},{8,4},{10,6},{12,0},{14,2},{1,13},{3,15... | collective-permute-start | bytes 393224 | tf_op jit(solution)/shard_map/ppermute | solution.py:275
  15.7 2.5 %query.1 = (bf16[5,256,128]{2,1,0:T(8,128)(2,1)S(1)}, f32[5,256,128]{2,1,0:T(8,128)S(1)}, f32[5,256,128]{2,1,0:T(8,128)S(1)}, bf16[256,560]{1,0:T(8,128)(2,1)}) custom-call(s32[1]{0:T(128)} %bitcast.row_ref, s32[1]{0:T(128)} %bitcast.1.place_ref, bf16[5,256,128]{2,1,0:T(8,128)(2,1)S(1)} %get-tuple-element.22.mixed_ref, ...), custom_call_target="tpu_custom_call" | custom-call | flops 167772160 | bytes 3956744 | tf_op jit(solution)/shard_map/query/pallas_call | solution.py:22
  18.2 4.8 %collective-permute-done.5.got_ref = bf16[512,128]{1,0:T(8,128)(2,1)S(1)} collective-permute-done((bf16[512,128]{1,0:T(8,128)(2,1)S(1)}, bf16[512,128]{1,0:T(8,128)(2,1)S(1)}, u32[]{:S(2)}, u32[]{:S(2)}) %collective-permute-start.5) | collective-permute-done | bytes 131104 | tf_op jit(solution)/shard_map/ppermute | solution.py:275
  23.0 1.5 %finish.1 = bf16[256,560]{1,0:T(8,128)(2,1)} custom-call(s32[1]{0:T(128)} %bitcast.row_ref, s32[1]{0:T(128)} %bitcast.1.place_ref, bf16[5,256,128]{2,1,0:T(8,128)(2,1)S(1)} %get-tuple-element.22.mixed_ref, bf16[5,256,128]{2,1,0:T(8,128)(2,1)S(1)} %get-tuple-element.29.q_ref, ...), custom_call_target="tpu_custom_call", output_to_operand_aliasing={{}: (7, {})} | custom-call | flops 41943040 | bytes 2670600 | tf_op jit(solution)/shard_map/finish/pallas_call | solution.py:22
Async XLA Ops:
  0.0 1.8 %collective-permute-start = (bf16[128,1120]{1,0:T(8,128)(2,1)}, bf16[128,1120]{1,0:T(8,128)(2,1)S(1)}, u32[]{:S(2)}, u32[]{:S(2)}) collective-permute-start(bf16[128,1120]{1,0:T(8,128)(2,1)} %bitcast.4), channel_id=1, source_target_pairs={{0,1},{1,0},{2,3},{3,2},{4,5},{5,4},{6,7},{7,6},{8,9},{9,8},{10,11... | collective-permute-start | bytes 860168 | tf_op jit(solution)/shard_map/ppermute | solution.py:315
  0.0 3.6 %copy-start = (bf16[4,10,112,112]{3,2,1,0:T(8,128)(2,1)S(1)}, bf16[4,10,112,112]{3,2,1,0:T(8,128)(2,1)}, u32[]{:S(2)}) copy-start(bf16[4,10,112,112]{3,2,1,0:T(8,128)(2,1)} %w_ref) | copy-start | bytes 3010564
  3.3 1.2 %collective-permute-start.1 = (f32[8,128]{1,0:T(8,128)S(1)}, f32[8,128]{1,0:T(8,128)S(1)}, u32[]{:S(2)}, u32[]{:S(2)}) collective-permute-start(f32[8,128]{1,0:T(8,128)S(1)} %get-tuple-element.24.part_ref), channel_id=1, source_target_pairs={{0,1},{1,0},{2,3},{3,2},{4,5},{5,4},{6,7},{7,6},{8,9},{9,8},{10,11... | collective-permute-start | bytes 12296 | tf_op jit(solution)/shard_map/ppermute | solution.py:330
  5.3 5.7 %collective-permute-start.4 = (bf16[512,128]{1,0:T(8,128)(2,1)S(1)}, bf16[512,128]{1,0:T(8,128)(2,1)S(1)}, u32[]{:S(2)}, u32[]{:S(2)}) collective-permute-start(bf16[512,128]{1,0:T(8,128)(2,1)S(1)} %get-tuple-element.28), channel_id=1, source_target_pairs={{0,2},{2,0},{4,6},{6,4},{8,10},{10,8},{12,14},{14,12},{1,3},{3,1},... | collective-permute-start | bytes 393224 | tf_op jit(solution)/shard_map/ppermute | solution.py:275
  6.9 6.4 %collective-permute-start.3 = (bf16[512,128]{1,0:T(8,128)(2,1)S(1)}, bf16[512,128]{1,0:T(8,128)(2,1)S(1)}, u32[]{:S(2)}, u32[]{:S(2)}) collective-permute-start(bf16[512,128]{1,0:T(8,128)(2,1)S(1)} %get-tuple-element.28), channel_id=1, source_target_pairs={{0,4},{2,6},{4,0},{6,2},{8,12},{10,14},{12,8},{14,10},{1,5},{3,7},... | collective-permute-start | bytes 393224 | tf_op jit(solution)/shard_map/ppermute | solution.py:275
  8.5 6.6 %collective-permute-start.2 = (bf16[512,128]{1,0:T(8,128)(2,1)S(1)}, bf16[512,128]{1,0:T(8,128)(2,1)S(1)}, u32[]{:S(2)}, u32[]{:S(2)}) collective-permute-start(bf16[512,128]{1,0:T(8,128)(2,1)S(1)} %get-tuple-element.28), channel_id=1, source_target_pairs={{0,6},{2,4},{4,2},{6,0},{8,14},{10,12},{12,10},{14,8},{1,7},{3,5},... | collective-permute-start | bytes 393224 | tf_op jit(solution)/shard_map/ppermute | solution.py:275
  15.1 7.8 %collective-permute-start.5 = (bf16[512,128]{1,0:T(8,128)(2,1)S(1)}, bf16[512,128]{1,0:T(8,128)(2,1)S(1)}, u32[]{:S(2)}, u32[]{:S(2)}) collective-permute-start(bf16[512,128]{1,0:T(8,128)(2,1)S(1)} %add_convert_fusion), channel_id=1, source_target_pairs={{0,12},{2,14},{4,8},{6,10},{8,4},{10,6},{12,0},{14,2},{1,13},{3,15... | collective-permute-start | bytes 393224 | tf_op jit(solution)/shard_map/ppermute | solution.py:275

commit v4 on v3

--- a/solution.py
+++ b/solution.py
@@ -55,7 +55,7 @@
             out_ref[h, :dim, m * LANES : (m + 1) * LANES] = block
 
 
-def split_heads(heads, dim, n_row, row, src_ref, u_ref, x_ref, at):
+def split_heads(heads, dim, n_row, row, src_ref, u_ref, x_ref):
     band, width = src_ref.shape
     full = src_ref[...].astype(F32)
     inv = lax.rsqrt(jnp.sum(full * full, axis=-1, keepdims=True) / width + 1e-06)
@@ -69,24 +69,33 @@
                 x = src_ref[:, lo : lo + dim]
                 if dim < LANES:
                     x = jnp.concatenate([x, jnp.zeros((band, LANES - dim), BF16)], axis=1)
-                x_ref[h, at, :] = x
-
-    for h in range(heads):
-        u_ref[h, at, :] = (x_ref[h, at, :].astype(F32) * inv).astype(BF16)
-
-
-def lead_kernel(heads, dim, n_row, row_ref, own_hbm, w_hbm, u_ref, x_ref, maps_ref, own_ref, w_ref, sems):
+                x_ref[h] = x
+
+    for h in range(heads):
+        u_ref[h] = (x_ref[h].astype(F32) * inv).astype(BF16)
+
+
+def project(heads, u_ref, maps_ref, q_ref, k_ref, v_ref, gate_ref):
+    for h in range(heads):
+        mapped = jnp.dot(u_ref[h], maps_ref[h], preferred_element_type=F32)
+        q_ref[h] = jnp.maximum(mapped[:, :LANES], 0.0).astype(BF16)
+        k_ref[h] = jnp.maximum(mapped[:, LANES : 2 * LANES], 0.0).astype(BF16)
+        v_ref[h] = mapped[:, 2 * LANES : 3 * LANES].astype(BF16)
+        gate_ref[h] = jax.nn.sigmoid(mapped[:, 3 * LANES :])
+
+
+def lead_kernel(
+    heads, dim, n_row, row_ref, own_hbm, w_hbm,
+    x_ref, q_ref, k_ref, v_ref, gate_ref, maps_ref, u_ref, own_ref, w_ref, sems,
+):
     row = row_ref[0]
     mine = pltpu.make_async_copy(own_hbm, own_ref, sems.at[w_hbm.shape[0]])
     mine.start()
     copies = fetch_maps(heads, row, w_hbm, w_ref, sems)
     mine.wait()
-    split_heads(heads, dim, n_row, row, own_ref, u_ref, x_ref, slice(None))
+    split_heads(heads, dim, n_row, row, own_ref, u_ref, x_ref)
     pack_maps(heads, 0, w_ref, maps_ref, copies)
-
-
-def pack_kernel(heads, row_ref, w_ref, maps_ref):
-    pack_maps(heads, row_ref[0] * heads, w_ref, maps_ref)
+    project(heads, u_ref, maps_ref, q_ref, k_ref, v_ref, gate_ref)
 
 
 def lane_blocks(sums, extra):
@@ -120,45 +129,48 @@
     return lax.dot_general(k, v, (((0,), (0,)), ((), ())), preferred_element_type=F32)
 
 
+def stacked(first_ref, then_ref, h):
+    return jnp.concatenate([first_ref[h], then_ref[h]], axis=0)
+
+
 def spatial_kernel(
-    heads, dim, n_row, row_ref, u_own_ref, x_own_ref, other_ref, w_ref,
+    heads, dim, n_row, row_ref, x_own_ref, q_own_ref, k_own_ref, v_own_ref, gate_own_ref, other_ref, maps_ref,
     mixed_ref, part_ref, u_ref, x_ref, q_ref, k_ref, v_ref, gate_ref, parts_ref,
 ):
     band = other_ref.shape[0]
-    split_heads(heads, dim, n_row, row_ref[0], other_ref, u_ref, x_ref, slice(None))
-    for h in range(heads):
-        u = jnp.concatenate([u_own_ref[h], u_ref[h]], axis=0)
-        mapped = jnp.dot(u, w_ref[h], preferred_element_type=F32)
-        q_ref[h] = jnp.maximum(mapped[:, :LANES], 0.0).astype(BF16)
-        k_ref[h] = jnp.maximum(mapped[:, LANES : 2 * LANES], 0.0).astype(BF16)
-        v_ref[h] = mapped[:, 2 * LANES : 3 * LANES].astype(BF16)
-        gate_ref[h] = jax.nn.sigmoid(mapped[:, 3 * LANES :])
-    for h in range(heads):
-        parts_ref[h] = split_state(outer_sum(k_ref[h], v_ref[h]))
+    split_heads(heads, dim, n_row, row_ref[0], other_ref, u_ref, x_ref)
+    project(heads, u_ref, maps_ref, q_ref, k_ref, v_ref, gate_ref)
+    for h in range(heads):
+        parts_ref[h] = split_state(outer_sum(stacked(k_own_ref, k_ref, h), stacked(v_own_ref, v_ref, h)))
     part = jnp.zeros((2 * band, LANES), F32)
     for h in range(heads):
-        x = jnp.concatenate([x_own_ref[h], x_ref[h]], axis=0).astype(F32)
-        mixed = finish(x, gate_ref[h], attend(q_ref[h], parts_ref[h]), dim)
+        attended = attend(stacked(q_own_ref, q_ref, h), parts_ref[h])
+        mixed = finish(stacked(x_own_ref, x_ref, h).astype(F32), stacked(gate_own_ref, gate_ref, h), attended, dim)
         mixed_ref[h] = mixed
         wide = mixed.astype(F32)
         part = part + wide * wide
     part_ref[...] = lane_blocks(jnp.sum(part, axis=-1, keepdims=True), band // SUBLANES)
 
 
-def state_kernel(heads, dim, width, mixed_ref, part_ref, got_ref, w_ref, u_ref, parts_ref, sent_ref, k_ref, v_ref):
-    blocks = mixed_ref.shape[1] // SUBLANES
+def token_scale(width, blocks, part_ref, got_ref):
     total = part_ref[...] + pltpu.roll(got_ref[...], LANES - blocks // 2, 1)
     tile = lax.rsqrt(total / width + 1e-06)
-    inv = jnp.concatenate([jnp.broadcast_to(tile[:, b : b + 1], (SUBLANES, LANES)) for b in range(blocks)], axis=0)
-    for h in range(heads):
-        u = (mixed_ref[h].astype(F32) * inv).astype(BF16)
-        u_ref[h] = u
-        mapped = jnp.dot(u, w_ref[h, :, LANES : 3 * LANES], preferred_element_type=F32)
-        k_ref[h] = jnp.maximum(mapped[:, :LANES], 0.0).astype(BF16)
-        v_ref[h] = mapped[:, LANES:].astype(BF16)
-    for h in range(heads):
-        state = outer_sum(k_ref[h], v_ref[h])
-        parts_ref[h] = split_state(state)
+    return jnp.concatenate([jnp.broadcast_to(tile[:, b : b + 1], (SUBLANES, LANES)) for b in range(blocks)], axis=0)
+
+
+def early_kernel(heads, row_ref, mixed_ref, w_ref, maps_ref, k_ref, v_ref):
+    pack_maps(heads, row_ref[0] * heads, w_ref, maps_ref)
+    for h in range(heads):
+        mapped = jnp.dot(mixed_ref[h], maps_ref[h, :, LANES : 3 * LANES], preferred_element_type=F32)
+        k_ref[h] = jnp.maximum(mapped[:, :LANES], 0.0)
+        v_ref[h] = mapped[:, LANES:]
+
+
+def state_kernel(heads, dim, width, k_ref, v_ref, part_ref, got_ref, state_ref, sent_ref):
+    inv = token_scale(width, k_ref.shape[1] // SUBLANES, part_ref, got_ref)
+    for h in range(heads):
+        state = outer_sum((k_ref[h] * inv).astype(BF16), (v_ref[h] * inv).astype(BF16))
+        state_ref[h] = state
         store_packed(sent_ref, h, heads, dim, state[:dim].astype(BF16))
 
 
@@ -226,24 +238,26 @@
         copy.wait()
 
 
-def query_kernel(heads, dim, n_row, taken, row_ref, place_ref, mixed_ref, u_ref, w_ref, parts_ref, *refs):
+def query_kernel(
+    heads, dim, width, n_row, taken, row_ref, place_ref, mixed_ref, part_ref, got_part_ref, maps_ref, state_ref, *refs
+):
     got_refs, (q_ref, gate_ref, base_ref, out_hbm, out_ref, sum_ref, tail_ref, sems) = refs[:-8], refs[-8:]
     place = place_ref[0]
-    if got_refs:
-        earlier = jnp.zeros(sum_ref.shape, F32)
-        for turn, got_ref in enumerate(got_refs):
-            earlier = earlier + jnp.where(taken(place, turn), got_ref[...].astype(F32), 0.0)
-        sum_ref[...] = earlier
-    for h in range(heads):
-        u = u_ref[h]
-        q = jnp.maximum(jnp.dot(u, w_ref[h, :, :LANES], preferred_element_type=F32), 0.0).astype(BF16)
+    earlier = jnp.zeros(sum_ref.shape, F32)
+    for turn, got_ref in enumerate(got_refs):
+        earlier = earlier + jnp.where(taken(place, turn), got_ref[...].astype(F32), 0.0)
+    sum_ref[...] = earlier
+    inv = token_scale(width, mixed_ref.shape[1] // SUBLANES, part_ref, got_part_ref)
+    for h in range(heads):
+        u = (mixed_ref[h].astype(F32) * inv).astype(BF16)
+        q = jnp.maximum(jnp.dot(u, maps_ref[h, :, :LANES], preferred_element_type=F32), 0.0).astype(BF16)
         q_ref[h] = q
-        gate_ref[h] = jax.nn.sigmoid(jnp.dot(u, w_ref[h, :, 3 * LANES :], preferred_element_type=F32))
-    for h in range(heads):
-        base = attend(q_ref[h], parts_ref[h])
+        gate_ref[h] = jax.nn.sigmoid(jnp.dot(u, maps_ref[h, :, 3 * LANES :], preferred_element_type=F32))
+    for h in range(heads):
+        state = state_ref[h]
         if got_refs:
-            base = base + attend(q_ref[h], split_state(load_packed(sum_ref, h, heads, dim, tail_ref)))
-        base_ref[h] = base
+            state = state + load_packed(sum_ref, h, heads, dim, tail_ref)
+        base_ref[h] = attend(q_ref[h], split_state(state))
     write_out(heads, dim, n_row, row_ref[0], mixed_ref, gate_ref, base_ref, out_hbm, out_ref, sems)
 
 
@@ -305,37 +319,39 @@
 
     packed_maps = shape(heads, LANES, maps * LANES)
     fetched = pltpu.VMEM((maps, heads, dim, dim), BF16)
-    per_head = pltpu.VMEM((heads, tokens, LANES), BF16)
     band_head = pltpu.VMEM((heads, band, LANES), BF16)
+    band_gates = pltpu.VMEM((heads, band, LANES), F32)
     gates = pltpu.VMEM((heads, tokens, LANES), F32)
+    own_outs = [shape(heads, band, LANES)] * 4 + [shape(heads, band, LANES, kind=F32)]
+    head_flops = 2 * tokens * heads * LANES * LANES
 
     own = latents.reshape(band, width)
     own_hbm = pltpu.with_memory_space_constraint(own, pltpu.HBM)
     spatial_weights = pltpu.with_memory_space_constraint(spatial_weights, pltpu.HBM)
     other = lax.ppermute(own, "row", swap)
-    u_own, x_own, maps_s = call(
-        functools.partial(lead_kernel, heads, dim, n_row), "lead",
-        [shape(heads, band, LANES), shape(heads, band, LANES), packed_maps],
+    *of_own, maps_s = call(
+        functools.partial(lead_kernel, heads, dim, n_row), "lead", own_outs + [packed_maps],
         [row, own_hbm, spatial_weights], [SMEM, HBM, HBM],
-        [pltpu.VMEM((band, width), BF16), fetched, pltpu.SemaphoreType.DMA((maps + 1,))],
+        [band_head, pltpu.VMEM((band, width), BF16), fetched, pltpu.SemaphoreType.DMA((maps + 1,))],
+        flops=head_flops * 2,
     )
     mixed, part = call(
         functools.partial(spatial_kernel, heads, dim, n_row), "spatial",
         [shape(heads, tokens, LANES), shape(SUBLANES, LANES, kind=F32)],
-        [row, u_own, x_own, other, maps_s], [SMEM] + [VMEM] * 4,
-        [band_head, band_head, per_head, per_head, per_head, gates, pltpu.VMEM((heads, 2 * LANES, LANES), BF16)],
-        flops=2 * tokens * heads * LANES * LANES * 6,
-    )
-    causal_weights, part = lax.optimization_barrier((causal_weights, part))
+        [row, *of_own, other, maps_s], [SMEM] + [VMEM] * 7,
+        [band_head] * 5 + [band_gates, pltpu.VMEM((heads, 2 * LANES, LANES), BF16)],
+        flops=head_flops * 4,
+    )
     got_part = lax.ppermute(part, "row", swap)
-    (maps_c,) = call(
-        functools.partial(pack_kernel, heads), "pack", [packed_maps], [row, causal_weights], [SMEM, VMEM],
-    )
-    u, parts, sent = call(
+    maps_c, k, v = call(
+        functools.partial(early_kernel, heads), "early",
+        [packed_maps] + [shape(heads, tokens, LANES, kind=F32)] * 2,
+        [row, mixed, causal_weights], [SMEM, VMEM, VMEM], flops=head_flops * 2,
+    )
+    state, sent = call(
         functools.partial(state_kernel, heads, dim, width), "state",
-        [shape(heads, tokens, LANES), shape(heads, 2 * LANES, LANES), shape(packed_rows(heads, dim), LANES)],
-        [mixed, part, got_part, maps_c], [VMEM] * 4, [per_head, per_head],
-        flops=2 * tokens * heads * LANES * LANES * 3,
+        [shape(heads, LANES, LANES, kind=F32), shape(packed_rows(heads, dim), LANES)],
+        [k, v, part, got_part], [VMEM] * 4, flops=head_flops,
     )
     got, taken = exchange_rounds(sent, "frame")
     packed_sum = pltpu.VMEM((packed_rows(heads, dim), LANES), F32)
@@ -343,17 +359,17 @@
     writing = [pltpu.VMEM((tokens, heads * dim), BF16)]
     done = [pltpu.SemaphoreType.DMA((n_row,))]
     q, gate, base, out = call(
-        functools.partial(query_kernel, heads, dim, n_row, taken), "query",
+        functools.partial(query_kernel, heads, dim, width, n_row, taken), "query",
         [shape(heads, tokens, LANES), shape(heads, tokens, LANES, kind=F32), shape(heads, tokens, LANES, kind=F32), whole],
-        [row, place, mixed, u, maps_c, parts, *got[:-1]], [SMEM] * 2 + [VMEM] * (3 + len(got)),
+        [row, place, mixed, part, got_part, maps_c, state, *got[:-1]], [SMEM] * 2 + [VMEM] * (4 + len(got)),
         writing + [packed_sum, pltpu.VMEM((LANES, LANES), F32)] + done,
-        flops=2 * tokens * heads * LANES * LANES * 4, out_specs=[VMEM] * 3 + [HBM],
+        flops=head_flops * 4, out_specs=[VMEM] * 3 + [HBM],
     )
     (out,) = call(
         functools.partial(finish_kernel, heads, dim, n_row, taken, len(got) - 1), "finish", [whole],
         [row, place, mixed, q, gate, base, got[-1], out], [SMEM] * 2 + [VMEM] * 5 + [HBM],
         writing + [pltpu.VMEM((heads, LANES, LANES), BF16), pltpu.VMEM((LANES, LANES), BF16), gates] + done,
-        flops=2 * tokens * heads * LANES * LANES, out_specs=[HBM], aliases={7: 0},
+        flops=head_flops, out_specs=[HBM], aliases={7: 0},
     )
     return out.reshape(frames, n_row * rows, cols, heads * dim)
 

time: 24.6 us -> 24.4 us (level)
  Pallas kernels: 7.81 us -> 7.23 us
    ppermute x4, waiting for transfers between devices: 11 us -> 11.7 us  [exchange_rounds(): lax.ppermute(sent, axis, [(i, i ^ mask) for i in range(size)])]
    pallas_call x6, Pallas kernels: 7.81 us -> 7.23 us  [call(): pl.pallas_call(kernel, name=name, out_shape=tuple(outs), in_specs=in_spec...]
    ppermute x1, waiting for transfers between devices: 0.81 us -> 0.43 us  [body(): got_part = lax.ppermute(part, 'row', swap)]
  transfers between devices with their start and end apart: 6 -> 6, of which waited for: 6 -> 6; matrix products, arithmetic and copies ran while one was open for 0% -> 0% of each run, Pallas kernels for 17% -> 16%
where the time goes in v4:
time: 24.4 us; the launch traced here: 24.2 us
  waiting for transfers between devices  12.2 us (50%)
  Pallas kernels  7.23 us (30%)
  starting transfers between devices  4.64 us (19%)
    ppermute x4, waiting for transfers between devices, exchange_rounds(): lax.ppermute(sent, axis, [(i, i ^ mask) for i in range(size)])  11.7 us
    pallas_call x6, Pallas kernels, call(): pl.pallas_call(kernel, name=name, out_shape=tuple(outs), in_specs=in_spec...  7.23 us
    ppermute x4, starting transfers between devices, exchange_rounds(): lax.ppermute(sent, axis, [(i, i ^ mask) for i in range(size)])  4.06 us
    ppermute x1, starting transfers between devices, body(): got_part = lax.ppermute(part, 'row', swap)  0.58 us
  transfers between devices with their start and end apart: 6, of which 6 were waited for; matrix products, arithmetic and copies ran while one was open for 0% of the time, Pallas kernels for 16%

profile of v4, /device:TPU:20, one launch (start us, length us, event | category | flops | bytes accessed | tf_op | source)
XLA Modules:
  0.0 24.2 jit_solution(14846688295716610257)
XLA Ops:
  0.0 0.0 collective-permute-start
  0.0 1.7 %lead.1 = (bf16[5,128,128]{2,1,0:T(8,128)(2,1)S(1)}, bf16[5,128,128]{2,1,0:T(8,128)(2,1)S(1)}, bf16[5,128,128]{2,1,0:T(8,128)(2,1)S(1)}, bf16[5,128,128]{2,1,0:T...) custom-call(s32[1]{0:T(128)} %bitcast.row_ref, bf16[128,1120]{1,0:T(8,128)(2,1)} %bitcast.5, ...), custom_call_target="tpu_custom_call" | custom-call | flops 83886080 | bytes 2928644 | tf_op jit(solution)/shard_map/lead/pallas_call | solution.py:22
  1.7 0.0 copy-start
  1.7 0.1 collective-permute-done.other_ref
  1.8 1.3 %spatial.1 = (bf16[5,256,128]{2,1,0:T(8,128)(2,1)S(1)}, f32[8,128]{1,0:T(8,128)S(1)}) custom-call(s32[1]{0:T(128)} %bitcast.row_ref, bf16[5,128,128]{2,1,0:T(8,128)(2,1)S(1)} %get-tuple-element.22.x_own_ref, bf16[5,128,128]{2,1,0:T(8,128)(2,1)S(1)} %get-tuple-element.23.q_own_ref, bf16[5,128,128]{2,1,0:T(8,128)(2,1)S(1)} %get-tuple-element.24.k_own_ref, ...), custom_call_target="tpu_custom_call" | custom-call | flops 167772160 | bytes 2256900 | tf_op jit(solution)/shard_map/spatial/pallas_call | solution.py:22
  3.1 0.6 %collective-permute-start.1 = (f32[8,128]{1,0:T(8,128)S(1)}, f32[8,128]{1,0:T(8,128)S(1)}, u32[]{:S(2)}, u32[]{:S(2)}) collective-permute-start(f32[8,128]{1,0:T(8,128)S(1)} %get-tuple-element.29.part_ref), channel_id=1, source_target_pairs={{0,1},{1,0},{2,3},{3,2},{4,5},{5,4},{6,7},{7,6},{8,9},{9,8},{10,11... | collective-permute-start | bytes 12296 | tf_op jit(solution)/shard_map/ppermute | solution.py:345
  3.7 0.0 copy-done
  3.7 0.4 %early.1 = (bf16[5,128,512]{2,1,0:T(8,128)(2,1)S(1)}, f32[5,256,128]{2,1,0:T(8,128)S(1)}, f32[5,256,128]{2,1,0:T(8,128)S(1)}) custom-call(s32[1]{0:T(128)} %bitcast.row_ref, bf16[5,256,128]{2,1,0:T(8,128)(2,1)S(1)} %get-tuple-element.28.mixed_ref, bf16[4,10,112,112]{3,2,1,0:T(8,128)(2,1)S(1)} %copy-done), custom_call_target="tpu_custom_call" | custom-call | flops 83886080 | bytes 3297284 | tf_op jit(solution)/shard_map/early/pallas_call | solution.py:22
  4.1 0.4 %collective-permute-done.1.got_ref.got_part_ref = f32[8,128]{1,0:T(8,128)S(1)} collective-permute-done((f32[8,128]{1,0:T(8,128)S(1)}, f32[8,128]{1,0:T(8,128)S(1)}, u32[]{:S(2)}, u32[]{:S(2)}) %collective-permute-start.1) | collective-permute-done | bytes 4128 | tf_op jit(solution)/shard_map/ppermute | solution.py:345
  4.5 0.5 %state.1 = (f32[5,128,128]{2,1,0:T(8,128)S(1)}, bf16[512,128]{1,0:T(8,128)(2,1)S(1)}) custom-call(f32[5,256,128]{2,1,0:T(8,128)S(1)} %get-tuple-element.31.k_ref, f32[5,256,128]{2,1,0:T(8,128)S(1)} %get-tuple-element.32.v_ref, f32[8,128]{1,0:T(8,128)S(1)} %get-tuple-element.29.part_ref, f32[8,128]{1,0:T(8,128)S(1)} %collective-permute-done.1.got_ref.got_part_ref), custom_call_target="tpu_custom_call" | custom-call | flops 41943040 | bytes 1777664 | tf_op jit(solution)/shard_map/state/pallas_call | solution.py:22
  5.1 1.5 %collective-permute-start.4 = (bf16[512,128]{1,0:T(8,128)(2,1)S(1)}, bf16[512,128]{1,0:T(8,128)(2,1)S(1)}, u32[]{:S(2)}, u32[]{:S(2)}) collective-permute-start(bf16[512,128]{1,0:T(8,128)(2,1)S(1)} %get-tuple-element.34), channel_id=1, source_target_pairs={{0,2},{2,0},{4,6},{6,4},{8,10},{10,8},{12,14},{14,12},{1,3},{3,1},... | collective-permute-start | bytes 393224 | tf_op jit(solution)/shard_map/ppermute | solution.py:289
  6.6 1.6 %collective-permute-start.3 = (bf16[512,128]{1,0:T(8,128)(2,1)S(1)}, bf16[512,128]{1,0:T(8,128)(2,1)S(1)}, u32[]{:S(2)}, u32[]{:S(2)}) collective-permute-start(bf16[512,128]{1,0:T(8,128)(2,1)S(1)} %get-tuple-element.34), channel_id=1, source_target_pairs={{0,4},{2,6},{4,0},{6,2},{8,12},{10,14},{12,8},{14,10},{1,5},{3,7},... | collective-permute-start | bytes 393224 | tf_op jit(solution)/shard_map/ppermute | solution.py:289
  8.2 0.4 %collective-permute-start.2 = (bf16[512,128]{1,0:T(8,128)(2,1)S(1)}, bf16[512,128]{1,0:T(8,128)(2,1)S(1)}, u32[]{:S(2)}, u32[]{:S(2)}) collective-permute-start(bf16[512,128]{1,0:T(8,128)(2,1)S(1)} %get-tuple-element.34), channel_id=1, source_target_pairs={{0,6},{2,4},{4,2},{6,0},{8,14},{10,12},{12,10},{14,8},{1,7},{3,5},... | collective-permute-start | bytes 393224 | tf_op jit(solution)/shard_map/ppermute | solution.py:289
  8.6 2.3 %collective-permute-done.4.refs_2_ = bf16[512,128]{1,0:T(8,128)(2,1)S(1)} collective-permute-done((bf16[512,128]{1,0:T(8,128)(2,1)S(1)}, bf16[512,128]{1,0:T(8,128)(2,1)S(1)}, u32[]{:S(2)}, u32[]{:S(2)}) %collective-permute-start.4) | collective-permute-done | bytes 131104 | tf_op jit(solution)/shard_map/ppermute | solution.py:289
  10.9 2.1 %collective-permute-done.3.refs_1_ = bf16[512,128]{1,0:T(8,128)(2,1)S(1)} collective-permute-done((bf16[512,128]{1,0:T(8,128)(2,1)S(1)}, bf16[512,128]{1,0:T(8,128)(2,1)S(1)}, u32[]{:S(2)}, u32[]{:S(2)}) %collective-permute-start.3) | collective-permute-done | bytes 131104 | tf_op jit(solution)/shard_map/ppermute | solution.py:289
  13.0 1.9 %collective-permute-done.2.refs_0_ = bf16[512,128]{1,0:T(8,128)(2,1)S(1)} collective-permute-done((bf16[512,128]{1,0:T(8,128)(2,1)S(1)}, bf16[512,128]{1,0:T(8,128)(2,1)S(1)}, u32[]{:S(2)}, u32[]{:S(2)}) %collective-permute-start.2) | collective-permute-done | bytes 131104 | tf_op jit(solution)/shard_map/ppermute | solution.py:289
  14.9 0.1 add_convert_fusion
  14.9 0.5 %collective-permute-start.5 = (bf16[512,128]{1,0:T(8,128)(2,1)S(1)}, bf16[512,128]{1,0:T(8,128)(2,1)S(1)}, u32[]{:S(2)}, u32[]{:S(2)}) collective-permute-start(bf16[512,128]{1,0:T(8,128)(2,1)S(1)} %add_convert_fusion), channel_id=1, source_target_pairs={{0,12},{2,14},{4,8},{6,10},{8,4},{10,6},{12,0},{14,2},{1,13},{3,15... | collective-permute-start | bytes 393224 | tf_op jit(solution)/shard_map/ppermute | solution.py:289
  15.4 1.9 %query.1 = (bf16[5,256,128]{2,1,0:T(8,128)(2,1)S(1)}, f32[5,256,128]{2,1,0:T(8,128)S(1)}, f32[5,256,128]{2,1,0:T(8,128)S(1)}, bf16[256,560]{1,0:T(8,128)(2,1)}) custom-call(s32[1]{0:T(128)} %bitcast.row_ref, s32[1]{0:T(128)} %bitcast.1.place_ref, bf16[5,256,128]{2,1,0:T(8,128)(2,1)S(1)} %get-tuple-element.28.mixed_ref, ...), custom_call_target="tpu_custom_call" | custom-call | flops 167772160 | bytes 3637256 | tf_op jit(solution)/shard_map/query/pallas_call | solution.py:22
  17.3 5.4 %collective-permute-done.5.got_ref = bf16[512,128]{1,0:T(8,128)(2,1)S(1)} collective-permute-done((bf16[512,128]{1,0:T(8,128)(2,1)S(1)}, bf16[512,128]{1,0:T(8,128)(2,1)S(1)}, u32[]{:S(2)}, u32[]{:S(2)}) %collective-permute-start.5) | collective-permute-done | bytes 131104 | tf_op jit(solution)/shard_map/ppermute | solution.py:289
  22.8 1.4 %finish.1 = bf16[256,560]{1,0:T(8,128)(2,1)} custom-call(s32[1]{0:T(128)} %bitcast.row_ref, s32[1]{0:T(128)} %bitcast.1.place_ref, bf16[5,256,128]{2,1,0:T(8,128)(2,1)S(1)} %get-tuple-element.28.mixed_ref, bf16[5,256,128]{2,1,0:T(8,128)(2,1)S(1)} %get-tuple-element.35.q_ref, ...), custom_call_target="tpu_custom_call", output_to_operand_aliasing={{}: (7, {})} | custom-call | flops 41943040 | bytes 2670600 | tf_op jit(solution)/shard_map/finish/pallas_call | solution.py:22
Async XLA Ops:
  0.0 1.8 %collective-permute-start = (bf16[128,1120]{1,0:T(8,128)(2,1)}, bf16[128,1120]{1,0:T(8,128)(2,1)S(1)}, u32[]{:S(2)}, u32[]{:S(2)}) collective-permute-start(bf16[128,1120]{1,0:T(8,128)(2,1)} %bitcast.4), channel_id=1, source_target_pairs={{0,1},{1,0},{2,3},{3,2},{4,5},{5,4},{6,7},{7,6},{8,9},{9,8},{10,11... | collective-permute-start | bytes 860168 | tf_op jit(solution)/shard_map/ppermute | solution.py:331
  1.7 2.0 %copy-start = (bf16[4,10,112,112]{3,2,1,0:T(8,128)(2,1)S(1)}, bf16[4,10,112,112]{3,2,1,0:T(8,128)(2,1)}, u32[]{:S(2)}) copy-start(bf16[4,10,112,112]{3,2,1,0:T(8,128)(2,1)} %w_ref.1) | copy-start | bytes 3010564
  3.1 1.4 %collective-permute-start.1 = (f32[8,128]{1,0:T(8,128)S(1)}, f32[8,128]{1,0:T(8,128)S(1)}, u32[]{:S(2)}, u32[]{:S(2)}) collective-permute-start(f32[8,128]{1,0:T(8,128)S(1)} %get-tuple-element.29.part_ref), channel_id=1, source_target_pairs={{0,1},{1,0},{2,3},{3,2},{4,5},{5,4},{6,7},{7,6},{8,9},{9,8},{10,11... | collective-permute-start | bytes 12296 | tf_op jit(solution)/shard_map/ppermute | solution.py:345
  5.1 5.8 %collective-permute-start.4 = (bf16[512,128]{1,0:T(8,128)(2,1)S(1)}, bf16[512,128]{1,0:T(8,128)(2,1)S(1)}, u32[]{:S(2)}, u32[]{:S(2)}) collective-permute-start(bf16[512,128]{1,0:T(8,128)(2,1)S(1)} %get-tuple-element.34), channel_id=1, source_target_pairs={{0,2},{2,0},{4,6},{6,4},{8,10},{10,8},{12,14},{14,12},{1,3},{3,1},... | collective-permute-start | bytes 393224 | tf_op jit(solution)/shard_map/ppermute | solution.py:289
  6.6 6.4 %collective-permute-start.3 = (bf16[512,128]{1,0:T(8,128)(2,1)S(1)}, bf16[512,128]{1,0:T(8,128)(2,1)S(1)}, u32[]{:S(2)}, u32[]{:S(2)}) collective-permute-start(bf16[512,128]{1,0:T(8,128)(2,1)S(1)} %get-tuple-element.34), channel_id=1, source_target_pairs={{0,4},{2,6},{4,0},{6,2},{8,12},{10,14},{12,8},{14,10},{1,5},{3,7},... | collective-permute-start | bytes 393224 | tf_op jit(solution)/shard_map/ppermute | solution.py:289
  8.2 6.7 %collective-permute-start.2 = (bf16[512,128]{1,0:T(8,128)(2,1)S(1)}, bf16[512,128]{1,0:T(8,128)(2,1)S(1)}, u32[]{:S(2)}, u32[]{:S(2)}) collective-permute-start(bf16[512,128]{1,0:T(8,128)(2,1)S(1)} %get-tuple-element.34), channel_id=1, source_target_pairs={{0,6},{2,4},{4,2},{6,0},{8,14},{10,12},{12,10},{14,8},{1,7},{3,5},... | collective-permute-start | bytes 393224 | tf_op jit(solution)/shard_map/ppermute | solution.py:289
  14.9 7.8 %collective-permute-start.5 = (bf16[512,128]{1,0:T(8,128)(2,1)S(1)}, bf16[512,128]{1,0:T(8,128)(2,1)S(1)}, u32[]{:S(2)}, u32[]{:S(2)}) collective-permute-start(bf16[512,128]{1,0:T(8,128)(2,1)S(1)} %add_convert_fusion), channel_id=1, source_target_pairs={{0,12},{2,14},{4,8},{6,10},{8,4},{10,6},{12,0},{14,2},{1,13},{3,15... | collective-permute-start | bytes 393224 | tf_op jit(solution)/shard_map/ppermute | solution.py:289

commit v5 on v4

--- a/solution.py
+++ b/solution.py
@@ -32,29 +32,6 @@
     )(*operands)
 
 
-def fetch_maps(heads, row, w_hbm, w_ref, sems):
-    first = row * heads
-    copies = []
-    for m in range(w_hbm.shape[0]):
-        copies.append(pltpu.make_async_copy(w_hbm.at[m, pl.ds(first, heads)], w_ref.at[m], sems.at[m]))
-        copies[-1].start()
-    return copies
-
-
-def pack_maps(heads, first, w_ref, out_ref, copies=()):
-    dim = w_ref.shape[2]
-    if dim < LANES:
-        out_ref[:, dim:, :] = jnp.zeros((heads, LANES - dim, out_ref.shape[2]), BF16)
-    for m in range(w_ref.shape[0]):
-        if copies:
-            copies[m].wait()
-        for h in range(heads):
-            block = w_ref[m, first + h]
-            if dim < LANES:
-                block = jnp.concatenate([block, jnp.zeros((dim, LANES - dim), BF16)], axis=1)
-            out_ref[h, :dim, m * LANES : (m + 1) * LANES] = block
-
-
 def split_heads(heads, dim, n_row, row, src_ref, u_ref, x_ref):
     band, width = src_ref.shape
     full = src_ref[...].astype(F32)
@@ -66,10 +43,7 @@
         def _():
             for h in range(heads):
                 lo = (r * heads + h) * dim
-                x = src_ref[:, lo : lo + dim]
-                if dim < LANES:
-                    x = jnp.concatenate([x, jnp.zeros((band, LANES - dim), BF16)], axis=1)
-                x_ref[h] = x
+                x_ref[h] = lanes_of(src_ref[:, lo : lo + dim])
 
     for h in range(heads):
         u_ref[h] = (x_ref[h].astype(F32) * inv).astype(BF16)
@@ -89,13 +63,33 @@
     x_ref, q_ref, k_ref, v_ref, gate_ref, maps_ref, u_ref, own_ref, w_ref, sems,
 ):
     row = row_ref[0]
-    mine = pltpu.make_async_copy(own_hbm, own_ref, sems.at[w_hbm.shape[0]])
+    mine = pltpu.make_async_copy(own_hbm, own_ref, sems.at[0])
     mine.start()
-    copies = fetch_maps(heads, row, w_hbm, w_ref, sems)
+    fetch = pltpu.make_async_copy(w_hbm.at[:, pl.ds(row * heads, heads)], w_ref, sems.at[1])
+    fetch.start()
+    clear_maps(heads, dim, maps_ref)
     mine.wait()
     split_heads(heads, dim, n_row, row, own_ref, u_ref, x_ref)
-    pack_maps(heads, 0, w_ref, maps_ref, copies)
+    fetch.wait()
+    for m in range(w_ref.shape[0]):
+        pack_map(heads, 0, m, w_ref, maps_ref)
     project(heads, u_ref, maps_ref, q_ref, k_ref, v_ref, gate_ref)
+
+
+def lanes_of(block):
+    rows, dim = block.shape
+    return jnp.concatenate([block, jnp.zeros((rows, LANES - dim), block.dtype)], axis=1) if dim < LANES else block
+
+
+def clear_maps(heads, dim, maps_ref):
+    if dim < LANES:
+        maps_ref[:, dim:, :] = jnp.zeros((heads, LANES - dim, maps_ref.shape[2]), BF16)
+
+
+def pack_map(heads, first, m, w_ref, maps_ref):
+    dim = w_ref.shape[2]
+    for h in range(heads):
+        maps_ref[h, :dim, m * LANES : (m + 1) * LANES] = lanes_of(w_ref[m, first + h])
 
 
 def lane_blocks(sums, extra):
@@ -159,7 +153,9 @@
 
 
 def early_kernel(heads, row_ref, mixed_ref, w_ref, maps_ref, k_ref, v_ref):
-    pack_maps(heads, row_ref[0] * heads, w_ref, maps_ref)
+    clear_maps(heads, w_ref.shape[2], maps_ref)
+    for m in range(w_ref.shape[0]):
+        pack_map(heads, row_ref[0] * heads, m, w_ref, maps_ref)
     for h in range(heads):
         mapped = jnp.dot(mixed_ref[h], maps_ref[h, :, LANES : 3 * LANES], preferred_element_type=F32)
         k_ref[h] = jnp.maximum(mapped[:, :LANES], 0.0)
@@ -177,8 +173,8 @@
 def packing(heads, dim):
     spare = LANES - dim
     if heads > 1 and spare and dim % spare == 0:
-        for left in range(dim - 16, 0, -16):
-            if (heads - 1) * (dim // left) >= dim // spare:
+        for left in range((dim - 1) // 16 * 16, 0, -16):
+            if dim // spare * left <= (heads - 1) * dim:
                 return dim - left
     return dim
 
@@ -188,12 +184,8 @@
 
 
 def spare_blocks(heads, dim):
-    kept = packing(heads, dim)
-    left, spare = dim - kept, LANES - dim
-    if not left:
-        return []
-    each = dim // left
-    return [((c // each) * dim + (c % each) * left, c * spare) for c in range(dim // spare)]
+    left, spare = dim - packing(heads, dim), LANES - dim
+    return [(c * left, c * spare) for c in range(dim // spare)] if left else []
 
 
 def store_packed(ref, h, heads, dim, block):
@@ -332,7 +324,7 @@
     *of_own, maps_s = call(
         functools.partial(lead_kernel, heads, dim, n_row), "lead", own_outs + [packed_maps],
         [row, own_hbm, spatial_weights], [SMEM, HBM, HBM],
-        [band_head, pltpu.VMEM((band, width), BF16), fetched, pltpu.SemaphoreType.DMA((maps + 1,))],
+        [band_head, pltpu.VMEM((band, width), BF16), fetched, pltpu.SemaphoreType.DMA((2,))],
         flops=head_flops * 2,
     )
     mixed, part = call(

time: 24.4 us -> 24 us (0.984)
    ppermute x4, waiting for transfers between devices: 11.7 us -> 11.4 us  [exchange_rounds(): lax.ppermute(sent, axis, [(i, i ^ mask) for i in range(size)])]
where the time goes in v5:
time: 24 us; the launch traced here: 23.9 us
  waiting for transfers between devices  12 us (50%)
  Pallas kernels  7.19 us (30%)
  starting transfers between devices  4.59 us (19%)
    ppermute x4, waiting for transfers between devices, exchange_rounds(): lax.ppermute(sent, axis, [(i, i ^ mask) for i in range(size)])  11.4 us
    pallas_call x6, Pallas kernels, call(): pl.pallas_call(kernel, name=name, out_shape=tuple(outs), in_specs=in_spec...  7.19 us
    ppermute x4, starting transfers between devices, exchange_rounds(): lax.ppermute(sent, axis, [(i, i ^ mask) for i in range(size)])  4.07 us
    ppermute x1, starting transfers between devices, body(): got_part = lax.ppermute(part, 'row', swap)  0.52 us
  transfers between devices with their start and end apart: 6, of which 6 were waited for; matrix products, arithmetic and copies ran while one was open for 0% of the time, Pallas kernels for 16%

profile of v5, /device:TPU:20, one launch (start us, length us, event | category | flops | bytes accessed | tf_op | source)
XLA Modules:
  0.0 23.9 jit_solution(9660650668681421963)
XLA Ops:
  0.0 0.0 collective-permute-start
  0.0 1.6 %lead.1 = (bf16[5,128,128]{2,1,0:T(8,128)(2,1)S(1)}, bf16[5,128,128]{2,1,0:T(8,128)(2,1)S(1)}, bf16[5,128,128]{2,1,0:T(8,128)(2,1)S(1)}, bf16[5,128,128]{2,1,0:T...) custom-call(s32[1]{0:T(128)} %bitcast.row_ref, bf16[128,1120]{1,0:T(8,128)(2,1)} %bitcast.5, ...), custom_call_target="tpu_custom_call" | custom-call | flops 83886080 | bytes 2928644 | tf_op jit(solution)/shard_map/lead/pallas_call | solution.py:22
  1.6 0.0 copy-start
  1.6 0.2 collective-permute-done.other_ref
  1.8 1.3 %spatial.1 = (bf16[5,256,128]{2,1,0:T(8,128)(2,1)S(1)}, f32[8,128]{1,0:T(8,128)S(1)}) custom-call(s32[1]{0:T(128)} %bitcast.row_ref, bf16[5,128,128]{2,1,0:T(8,128)(2,1)S(1)} %get-tuple-element.22.x_own_ref, bf16[5,128,128]{2,1,0:T(8,128)(2,1)S(1)} %get-tuple-element.23.q_own_ref, bf16[5,128,128]{2,1,0:T(8,128)(2,1)S(1)} %get-tuple-element.24.k_own_ref, ...), custom_call_target="tpu_custom_call" | custom-call | flops 167772160 | bytes 2256900 | tf_op jit(solution)/shard_map/spatial/pallas_call | solution.py:22
  3.1 0.5 %collective-permute-start.1 = (f32[8,128]{1,0:T(8,128)S(1)}, f32[8,128]{1,0:T(8,128)S(1)}, u32[]{:S(2)}, u32[]{:S(2)}) collective-permute-start(f32[8,128]{1,0:T(8,128)S(1)} %get-tuple-element.29.part_ref), channel_id=1, source_target_pairs={{0,1},{1,0},{2,3},{3,2},{4,5},{5,4},{6,7},{7,6},{8,9},{9,8},{10,11... | collective-permute-start | bytes 12296 | tf_op jit(solution)/shard_map/ppermute | solution.py:337
  3.6 0.0 copy-done
  3.6 0.4 %early.1 = (bf16[5,128,512]{2,1,0:T(8,128)(2,1)S(1)}, f32[5,256,128]{2,1,0:T(8,128)S(1)}, f32[5,256,128]{2,1,0:T(8,128)S(1)}) custom-call(s32[1]{0:T(128)} %bitcast.row_ref, bf16[5,256,128]{2,1,0:T(8,128)(2,1)S(1)} %get-tuple-element.28.mixed_ref, bf16[4,10,112,112]{3,2,1,0:T(8,128)(2,1)S(1)} %copy-done), custom_call_target="tpu_custom_call" | custom-call | flops 83886080 | bytes 3297284 | tf_op jit(solution)/shard_map/early/pallas_call | solution.py:22
  4.0 0.4 %collective-permute-done.1.got_ref.got_part_ref = f32[8,128]{1,0:T(8,128)S(1)} collective-permute-done((f32[8,128]{1,0:T(8,128)S(1)}, f32[8,128]{1,0:T(8,128)S(1)}, u32[]{:S(2)}, u32[]{:S(2)}) %collective-permute-start.1) | collective-permute-done | bytes 4128 | tf_op jit(solution)/shard_map/ppermute | solution.py:337
  4.4 0.6 %state.1 = (f32[5,128,128]{2,1,0:T(8,128)S(1)}, bf16[496,128]{1,0:T(8,128)(2,1)S(1)}) custom-call(f32[5,256,128]{2,1,0:T(8,128)S(1)} %get-tuple-element.31.k_ref, f32[5,256,128]{2,1,0:T(8,128)S(1)} %get-tuple-element.32.v_ref, f32[8,128]{1,0:T(8,128)S(1)} %get-tuple-element.29.part_ref, f32[8,128]{1,0:T(8,128)S(1)} %collective-permute-done.1.got_ref.got_part_ref), custom_call_target="tpu_custom_call" | custom-call | flops 41943040 | bytes 1773568 | tf_op jit(solution)/shard_map/state/pallas_call | solution.py:22
  5.0 1.6 %collective-permute-start.4 = (bf16[496,128]{1,0:T(8,128)(2,1)S(1)}, bf16[496,128]{1,0:T(8,128)(2,1)S(1)}, u32[]{:S(2)}, u32[]{:S(2)}) collective-permute-start(bf16[496,128]{1,0:T(8,128)(2,1)S(1)} %get-tuple-element.34), channel_id=1, source_target_pairs={{0,2},{2,0},{4,6},{6,4},{8,10},{10,8},{12,14},{14,12},{1,3},{3,1},... | collective-permute-start | bytes 380936 | tf_op jit(solution)/shard_map/ppermute | solution.py:281
  6.6 1.6 %collective-permute-start.3 = (bf16[496,128]{1,0:T(8,128)(2,1)S(1)}, bf16[496,128]{1,0:T(8,128)(2,1)S(1)}, u32[]{:S(2)}, u32[]{:S(2)}) collective-permute-start(bf16[496,128]{1,0:T(8,128)(2,1)S(1)} %get-tuple-element.34), channel_id=1, source_target_pairs={{0,4},{2,6},{4,0},{6,2},{8,12},{10,14},{12,8},{14,10},{1,5},{3,7},... | collective-permute-start | bytes 380936 | tf_op jit(solution)/shard_map/ppermute | solution.py:281
  8.1 0.4 %collective-permute-start.2 = (bf16[496,128]{1,0:T(8,128)(2,1)S(1)}, bf16[496,128]{1,0:T(8,128)(2,1)S(1)}, u32[]{:S(2)}, u32[]{:S(2)}) collective-permute-start(bf16[496,128]{1,0:T(8,128)(2,1)S(1)} %get-tuple-element.34), channel_id=1, source_target_pairs={{0,6},{2,4},{4,2},{6,0},{8,14},{10,12},{12,10},{14,8},{1,7},{3,5},... | collective-permute-start | bytes 380936 | tf_op jit(solution)/shard_map/ppermute | solution.py:281
  8.6 2.2 %collective-permute-done.4.refs_2_ = bf16[496,128]{1,0:T(8,128)(2,1)S(1)} collective-permute-done((bf16[496,128]{1,0:T(8,128)(2,1)S(1)}, bf16[496,128]{1,0:T(8,128)(2,1)S(1)}, u32[]{:S(2)}, u32[]{:S(2)}) %collective-permute-start.4) | collective-permute-done | bytes 127008 | tf_op jit(solution)/shard_map/ppermute | solution.py:281
  10.7 2.1 %collective-permute-done.3.refs_1_ = bf16[496,128]{1,0:T(8,128)(2,1)S(1)} collective-permute-done((bf16[496,128]{1,0:T(8,128)(2,1)S(1)}, bf16[496,128]{1,0:T(8,128)(2,1)S(1)}, u32[]{:S(2)}, u32[]{:S(2)}) %collective-permute-start.3) | collective-permute-done | bytes 127008 | tf_op jit(solution)/shard_map/ppermute | solution.py:281
  12.8 1.8 %collective-permute-done.2.refs_0_ = bf16[496,128]{1,0:T(8,128)(2,1)S(1)} collective-permute-done((bf16[496,128]{1,0:T(8,128)(2,1)S(1)}, bf16[496,128]{1,0:T(8,128)(2,1)S(1)}, u32[]{:S(2)}, u32[]{:S(2)}) %collective-permute-start.2) | collective-permute-done | bytes 127008 | tf_op jit(solution)/shard_map/ppermute | solution.py:281
  14.6 0.1 add_convert_fusion
  14.7 0.5 %collective-permute-start.5 = (bf16[496,128]{1,0:T(8,128)(2,1)S(1)}, bf16[496,128]{1,0:T(8,128)(2,1)S(1)}, u32[]{:S(2)}, u32[]{:S(2)}) collective-permute-start(bf16[496,128]{1,0:T(8,128)(2,1)S(1)} %add_convert_fusion), channel_id=1, source_target_pairs={{0,12},{2,14},{4,8},{6,10},{8,4},{10,6},{12,0},{14,2},{1,13},{3,15... | collective-permute-start | bytes 380936 | tf_op jit(solution)/shard_map/ppermute | solution.py:281
  15.2 1.9 %query.1 = (bf16[5,256,128]{2,1,0:T(8,128)(2,1)S(1)}, f32[5,256,128]{2,1,0:T(8,128)S(1)}, f32[5,256,128]{2,1,0:T(8,128)S(1)}, bf16[256,560]{1,0:T(8,128)(2,1)}) custom-call(s32[1]{0:T(128)} %bitcast.row_ref, s32[1]{0:T(128)} %bitcast.1.place_ref, bf16[5,256,128]{2,1,0:T(8,128)(2,1)S(1)} %get-tuple-element.28.mixed_ref, ...), custom_call_target="tpu_custom_call" | custom-call | flops 167772160 | bytes 3624968 | tf_op jit(solution)/shard_map/query/pallas_call | solution.py:22
  17.1 5.3 %collective-permute-done.5.got_ref = bf16[496,128]{1,0:T(8,128)(2,1)S(1)} collective-permute-done((bf16[496,128]{1,0:T(8,128)(2,1)S(1)}, bf16[496,128]{1,0:T(8,128)(2,1)S(1)}, u32[]{:S(2)}, u32[]{:S(2)}) %collective-permute-start.5) | collective-permute-done | bytes 127008 | tf_op jit(solution)/shard_map/ppermute | solution.py:281
  22.4 1.5 %finish.1 = bf16[256,560]{1,0:T(8,128)(2,1)} custom-call(s32[1]{0:T(128)} %bitcast.row_ref, s32[1]{0:T(128)} %bitcast.1.place_ref, bf16[5,256,128]{2,1,0:T(8,128)(2,1)S(1)} %get-tuple-element.28.mixed_ref, bf16[5,256,128]{2,1,0:T(8,128)(2,1)S(1)} %get-tuple-element.35.q_ref, ...), custom_call_target="tpu_custom_call", output_to_operand_aliasing={{}: (7, {})} | custom-call | flops 41943040 | bytes 2666504 | tf_op jit(solution)/shard_map/finish/pallas_call | solution.py:22
Async XLA Ops:
  0.0 1.8 %collective-permute-start = (bf16[128,1120]{1,0:T(8,128)(2,1)}, bf16[128,1120]{1,0:T(8,128)(2,1)S(1)}, u32[]{:S(2)}, u32[]{:S(2)}) collective-permute-start(bf16[128,1120]{1,0:T(8,128)(2,1)} %bitcast.4), channel_id=1, source_target_pairs={{0,1},{1,0},{2,3},{3,2},{4,5},{5,4},{6,7},{7,6},{8,9},{9,8},{10,11... | collective-permute-start | bytes 860168 | tf_op jit(solution)/shard_map/ppermute | solution.py:323
  1.6 2.0 %copy-start = (bf16[4,10,112,112]{3,2,1,0:T(8,128)(2,1)S(1)}, bf16[4,10,112,112]{3,2,1,0:T(8,128)(2,1)}, u32[]{:S(2)}) copy-start(bf16[4,10,112,112]{3,2,1,0:T(8,128)(2,1)} %w_ref.1) | copy-start | bytes 3010564
  3.1 1.3 %collective-permute-start.1 = (f32[8,128]{1,0:T(8,128)S(1)}, f32[8,128]{1,0:T(8,128)S(1)}, u32[]{:S(2)}, u32[]{:S(2)}) collective-permute-start(f32[8,128]{1,0:T(8,128)S(1)} %get-tuple-element.29.part_ref), channel_id=1, source_target_pairs={{0,1},{1,0},{2,3},{3,2},{4,5},{5,4},{6,7},{7,6},{8,9},{9,8},{10,11... | collective-permute-start | bytes 12296 | tf_op jit(solution)/shard_map/ppermute | solution.py:337
  5.0 5.7 %collective-permute-start.4 = (bf16[496,128]{1,0:T(8,128)(2,1)S(1)}, bf16[496,128]{1,0:T(8,128)(2,1)S(1)}, u32[]{:S(2)}, u32[]{:S(2)}) collective-permute-start(bf16[496,128]{1,0:T(8,128)(2,1)S(1)} %get-tuple-element.34), channel_id=1, source_target_pairs={{0,2},{2,0},{4,6},{6,4},{8,10},{10,8},{12,14},{14,12},{1,3},{3,1},... | collective-permute-start | bytes 380936 | tf_op jit(solution)/shard_map/ppermute | solution.py:281
  6.6 6.3 %collective-permute-start.3 = (bf16[496,128]{1,0:T(8,128)(2,1)S(1)}, bf16[496,128]{1,0:T(8,128)(2,1)S(1)}, u32[]{:S(2)}, u32[]{:S(2)}) collective-permute-start(bf16[496,128]{1,0:T(8,128)(2,1)S(1)} %get-tuple-element.34), channel_id=1, source_target_pairs={{0,4},{2,6},{4,0},{6,2},{8,12},{10,14},{12,8},{14,10},{1,5},{3,7},... | collective-permute-start | bytes 380936 | tf_op jit(solution)/shard_map/ppermute | solution.py:281
  8.1 6.5 %collective-permute-start.2 = (bf16[496,128]{1,0:T(8,128)(2,1)S(1)}, bf16[496,128]{1,0:T(8,128)(2,1)S(1)}, u32[]{:S(2)}, u32[]{:S(2)}) collective-permute-start(bf16[496,128]{1,0:T(8,128)(2,1)S(1)} %get-tuple-element.34), channel_id=1, source_target_pairs={{0,6},{2,4},{4,2},{6,0},{8,14},{10,12},{12,10},{14,8},{1,7},{3,5},... | collective-permute-start | bytes 380936 | tf_op jit(solution)/shard_map/ppermute | solution.py:281
  14.7 7.7 %collective-permute-start.5 = (bf16[496,128]{1,0:T(8,128)(2,1)S(1)}, bf16[496,128]{1,0:T(8,128)(2,1)S(1)}, u32[]{:S(2)}, u32[]{:S(2)}) collective-permute-start(bf16[496,128]{1,0:T(8,128)(2,1)S(1)} %add_convert_fusion), channel_id=1, source_target_pairs={{0,12},{2,14},{4,8},{6,10},{8,4},{10,6},{12,0},{14,2},{1,13},{3,15... | collective-permute-start | bytes 380936 | tf_op jit(solution)/shard_map/ppermute | solution.py:281

commit v6 on v5

--- a/solution.py
+++ b/solution.py
@@ -51,11 +51,13 @@
 
 def project(heads, u_ref, maps_ref, q_ref, k_ref, v_ref, gate_ref):
     for h in range(heads):
-        mapped = jnp.dot(u_ref[h], maps_ref[h], preferred_element_type=F32)
-        q_ref[h] = jnp.maximum(mapped[:, :LANES], 0.0).astype(BF16)
-        k_ref[h] = jnp.maximum(mapped[:, LANES : 2 * LANES], 0.0).astype(BF16)
-        v_ref[h] = mapped[:, 2 * LANES : 3 * LANES].astype(BF16)
-        gate_ref[h] = jax.nn.sigmoid(mapped[:, 3 * LANES :])
+        mapped = jnp.dot(u_ref[h], maps_ref[h, :, LANES : 3 * LANES], preferred_element_type=F32)
+        k_ref[h] = jnp.maximum(mapped[:, :LANES], 0.0).astype(BF16)
+        v_ref[h] = mapped[:, LANES:].astype(BF16)
+    for h in range(heads):
+        u = u_ref[h]
+        q_ref[h] = jnp.maximum(jnp.dot(u, maps_ref[h, :, :LANES], preferred_element_type=F32), 0.0).astype(BF16)
+        gate_ref[h] = jax.nn.sigmoid(jnp.dot(u, maps_ref[h, :, 3 * LANES :], preferred_element_type=F32))
 
 
 def lead_kernel(
@@ -216,15 +218,19 @@
     return block
 
 
-def write_out(heads, dim, n_row, row, mixed_ref, gate_ref, attended_ref, out_hbm, out_ref, sems):
+def write_out(heads, dim, n_row, row, mixed_ref, gate_ref, attended_ref, scaled_ref, out_hbm, out_ref, sems):
     band = mixed_ref.shape[1] // n_row
     for h in range(heads):
-        new = finish(mixed_ref[h].astype(F32), gate_ref[h], attended_ref[h], dim)
-        out_ref[:, h * dim : (h + 1) * dim] = new[:, :dim]
+        attended = attended_ref[h]
+        scaled_ref[h] = attended * lax.rsqrt(jnp.sum(attended * attended, axis=-1, keepdims=True) / dim + 1e-05)
     copies = []
     for b, place in enumerate((row, n_row - 1 - row)):
+        at = slice(b * band, (b + 1) * band)
+        for h in range(heads):
+            new = (mixed_ref[h, at, :].astype(F32) + gate_ref[h, at, :] * scaled_ref[h, at, :]).astype(BF16)
+            out_ref[at, h * dim : (h + 1) * dim] = new[:, :dim]
         to = pl.ds(pl.multiple_of(place * band, band), band)
-        copies.append(pltpu.make_async_copy(out_ref.at[b * band : (b + 1) * band], out_hbm.at[to], sems.at[b]))
+        copies.append(pltpu.make_async_copy(out_ref.at[at], out_hbm.at[to], sems.at[b]))
         copies[-1].start()
     for copy in copies:
         copy.wait()
@@ -233,7 +239,7 @@
 def query_kernel(
     heads, dim, width, n_row, taken, row_ref, place_ref, mixed_ref, part_ref, got_part_ref, maps_ref, state_ref, *refs
 ):
-    got_refs, (q_ref, gate_ref, base_ref, out_hbm, out_ref, sum_ref, tail_ref, sems) = refs[:-8], refs[-8:]
+    got_refs, (q_ref, gate_ref, base_ref, out_hbm, out_ref, scaled_ref, sum_ref, tail_ref, sems) = refs[:-9], refs[-9:]
     place = place_ref[0]
     earlier = jnp.zeros(sum_ref.shape, F32)
     for turn, got_ref in enumerate(got_refs):
@@ -250,7 +256,7 @@
         if got_refs:
             state = state + load_packed(sum_ref, h, heads, dim, tail_ref)
         base_ref[h] = attend(q_ref[h], split_state(state))
-    write_out(heads, dim, n_row, row_ref[0], mixed_ref, gate_ref, base_ref, out_hbm, out_ref, sems)
+    write_out(heads, dim, n_row, row_ref[0], mixed_ref, gate_ref, base_ref, scaled_ref, out_hbm, out_ref, sems)
 
 
 def finish_kernel(
@@ -263,7 +269,9 @@
             state_ref[h] = load_packed(got_ref, h, heads, dim, tail_ref).astype(BF16)
         for h in range(heads):
             attended_ref[h] = base_ref[h] + jnp.dot(q_ref[h], state_ref[h], preferred_element_type=F32)
-        write_out(heads, dim, n_row, row_ref[0], mixed_ref, gate_ref, attended_ref, out_hbm, out_ref, sems)
+        write_out(
+            heads, dim, n_row, row_ref[0], mixed_ref, gate_ref, attended_ref, attended_ref, out_hbm, out_ref, sems
+        )
 
 
 def exchange_rounds(sent, axis):
@@ -354,7 +362,7 @@
         functools.partial(query_kernel, heads, dim, width, n_row, taken), "query",
         [shape(heads, tokens, LANES), shape(heads, tokens, LANES, kind=F32), shape(heads, tokens, LANES, kind=F32), whole],
         [row, place, mixed, part, got_part, maps_c, state, *got[:-1]], [SMEM] * 2 + [VMEM] * (4 + len(got)),
-        writing + [packed_sum, pltpu.VMEM((LANES, LANES), F32)] + done,
+        writing + [gates, packed_sum, pltpu.VMEM((LANES, LANES), F32)] + done,
         flops=head_flops * 4, out_specs=[VMEM] * 3 + [HBM],
     )
     (out,) = call(

time: 24 us -> 23.8 us (level)
  Pallas kernels: 7.19 us -> 6.92 us
    pallas_call x6, Pallas kernels: 7.19 us -> 6.92 us  [call(): pl.pallas_call(kernel, name=name, out_shape=tuple(outs), in_specs=in_spec...]
where the time goes in v6:
time: 23.8 us; the launch traced here: 23.6 us
  waiting for transfers between devices  12 us (50%)
  Pallas kernels  6.92 us (29%)
  starting transfers between devices  4.6 us (19%)
    ppermute x4, waiting for transfers between devices, exchange_rounds(): lax.ppermute(sent, axis, [(i, i ^ mask) for i in range(size)])  11.4 us
    pallas_call x6, Pallas kernels, call(): pl.pallas_call(kernel, name=name, out_shape=tuple(outs), in_specs=in_spec...  6.92 us
    ppermute x4, starting transfers between devices, exchange_rounds(): lax.ppermute(sent, axis, [(i, i ^ mask) for i in range(size)])  4.07 us
    ppermute x1, starting transfers between devices, body(): got_part = lax.ppermute(part, 'row', swap)  0.53 us
  transfers between devices with their start and end apart: 6, of which 6 were waited for; matrix products, arithmetic and copies ran while one was open for 0% of the time, Pallas kernels for 16%

profile of v6, /device:TPU:20, one launch (start us, length us, event | category | flops | bytes accessed | tf_op | source)
XLA Modules:
  0.0 23.6 jit_solution(13676566444619898559)
XLA Ops:
  0.0 0.0 collective-permute-start
  0.0 1.6 %lead.1 = (bf16[5,128,128]{2,1,0:T(8,128)(2,1)S(1)}, bf16[5,128,128]{2,1,0:T(8,128)(2,1)S(1)}, bf16[5,128,128]{2,1,0:T(8,128)(2,1)S(1)}, bf16[5,128,128]{2,1,0:T...) custom-call(s32[1]{0:T(128)} %bitcast.row_ref, bf16[128,1120]{1,0:T(8,128)(2,1)} %bitcast.5, ...), custom_call_target="tpu_custom_call" | custom-call | flops 83886080 | bytes 2928644 | tf_op jit(solution)/shard_map/lead/pallas_call | solution.py:22
  1.6 0.0 copy-start
  1.7 0.1 collective-permute-done.other_ref
  1.8 1.2 %spatial.1 = (bf16[5,256,128]{2,1,0:T(8,128)(2,1)S(1)}, f32[8,128]{1,0:T(8,128)S(1)}) custom-call(s32[1]{0:T(128)} %bitcast.row_ref, bf16[5,128,128]{2,1,0:T(8,128)(2,1)S(1)} %get-tuple-element.22.x_own_ref, bf16[5,128,128]{2,1,0:T(8,128)(2,1)S(1)} %get-tuple-element.23.q_own_ref, bf16[5,128,128]{2,1,0:T(8,128)(2,1)S(1)} %get-tuple-element.24.k_own_ref, ...), custom_call_target="tpu_custom_call" | custom-call | flops 167772160 | bytes 2256900 | tf_op jit(solution)/shard_map/spatial/pallas_call | solution.py:22
  3.0 0.5 %collective-permute-start.1 = (f32[8,128]{1,0:T(8,128)S(1)}, f32[8,128]{1,0:T(8,128)S(1)}, u32[]{:S(2)}, u32[]{:S(2)}) collective-permute-start(f32[8,128]{1,0:T(8,128)S(1)} %get-tuple-element.29.part_ref), channel_id=1, source_target_pairs={{0,1},{1,0},{2,3},{3,2},{4,5},{5,4},{6,7},{7,6},{8,9},{9,8},{10,11... | collective-permute-start | bytes 12296 | tf_op jit(solution)/shard_map/ppermute | solution.py:345
  3.6 0.0 copy-done
  3.6 0.4 %early.1 = (bf16[5,128,512]{2,1,0:T(8,128)(2,1)S(1)}, f32[5,256,128]{2,1,0:T(8,128)S(1)}, f32[5,256,128]{2,1,0:T(8,128)S(1)}) custom-call(s32[1]{0:T(128)} %bitcast.row_ref, bf16[5,256,128]{2,1,0:T(8,128)(2,1)S(1)} %get-tuple-element.28.mixed_ref, bf16[4,10,112,112]{3,2,1,0:T(8,128)(2,1)S(1)} %copy-done), custom_call_target="tpu_custom_call" | custom-call | flops 83886080 | bytes 3297284 | tf_op jit(solution)/shard_map/early/pallas_call | solution.py:22
  4.0 0.4 %collective-permute-done.1.got_ref.got_part_ref = f32[8,128]{1,0:T(8,128)S(1)} collective-permute-done((f32[8,128]{1,0:T(8,128)S(1)}, f32[8,128]{1,0:T(8,128)S(1)}, u32[]{:S(2)}, u32[]{:S(2)}) %collective-permute-start.1) | collective-permute-done | bytes 4128 | tf_op jit(solution)/shard_map/ppermute | solution.py:345
  4.4 0.6 %state.1 = (f32[5,128,128]{2,1,0:T(8,128)S(1)}, bf16[496,128]{1,0:T(8,128)(2,1)S(1)}) custom-call(f32[5,256,128]{2,1,0:T(8,128)S(1)} %get-tuple-element.31.k_ref, f32[5,256,128]{2,1,0:T(8,128)S(1)} %get-tuple-element.32.v_ref, f32[8,128]{1,0:T(8,128)S(1)} %get-tuple-element.29.part_ref, f32[8,128]{1,0:T(8,128)S(1)} %collective-permute-done.1.got_ref.got_part_ref), custom_call_target="tpu_custom_call" | custom-call | flops 41943040 | bytes 1773568 | tf_op jit(solution)/shard_map/state/pallas_call | solution.py:22
  4.9 1.6 %collective-permute-start.4 = (bf16[496,128]{1,0:T(8,128)(2,1)S(1)}, bf16[496,128]{1,0:T(8,128)(2,1)S(1)}, u32[]{:S(2)}, u32[]{:S(2)}) collective-permute-start(bf16[496,128]{1,0:T(8,128)(2,1)S(1)} %get-tuple-element.34), channel_id=1, source_target_pairs={{0,2},{2,0},{4,6},{6,4},{8,10},{10,8},{12,14},{14,12},{1,3},{3,1},... | collective-permute-start | bytes 380936 | tf_op jit(solution)/shard_map/ppermute | solution.py:289
  6.5 1.6 %collective-permute-start.3 = (bf16[496,128]{1,0:T(8,128)(2,1)S(1)}, bf16[496,128]{1,0:T(8,128)(2,1)S(1)}, u32[]{:S(2)}, u32[]{:S(2)}) collective-permute-start(bf16[496,128]{1,0:T(8,128)(2,1)S(1)} %get-tuple-element.34), channel_id=1, source_target_pairs={{0,4},{2,6},{4,0},{6,2},{8,12},{10,14},{12,8},{14,10},{1,5},{3,7},... | collective-permute-start | bytes 380936 | tf_op jit(solution)/shard_map/ppermute | solution.py:289
  8.1 0.4 %collective-permute-start.2 = (bf16[496,128]{1,0:T(8,128)(2,1)S(1)}, bf16[496,128]{1,0:T(8,128)(2,1)S(1)}, u32[]{:S(2)}, u32[]{:S(2)}) collective-permute-start(bf16[496,128]{1,0:T(8,128)(2,1)S(1)} %get-tuple-element.34), channel_id=1, source_target_pairs={{0,6},{2,4},{4,2},{6,0},{8,14},{10,12},{12,10},{14,8},{1,7},{3,5},... | collective-permute-start | bytes 380936 | tf_op jit(solution)/shard_map/ppermute | solution.py:289
  8.5 2.2 %collective-permute-done.4.refs_2_ = bf16[496,128]{1,0:T(8,128)(2,1)S(1)} collective-permute-done((bf16[496,128]{1,0:T(8,128)(2,1)S(1)}, bf16[496,128]{1,0:T(8,128)(2,1)S(1)}, u32[]{:S(2)}, u32[]{:S(2)}) %collective-permute-start.4) | collective-permute-done | bytes 127008 | tf_op jit(solution)/shard_map/ppermute | solution.py:289
  10.7 2.1 %collective-permute-done.3.refs_1_ = bf16[496,128]{1,0:T(8,128)(2,1)S(1)} collective-permute-done((bf16[496,128]{1,0:T(8,128)(2,1)S(1)}, bf16[496,128]{1,0:T(8,128)(2,1)S(1)}, u32[]{:S(2)}, u32[]{:S(2)}) %collective-permute-start.3) | collective-permute-done | bytes 127008 | tf_op jit(solution)/shard_map/ppermute | solution.py:289
  12.8 1.8 %collective-permute-done.2.refs_0_ = bf16[496,128]{1,0:T(8,128)(2,1)S(1)} collective-permute-done((bf16[496,128]{1,0:T(8,128)(2,1)S(1)}, bf16[496,128]{1,0:T(8,128)(2,1)S(1)}, u32[]{:S(2)}, u32[]{:S(2)}) %collective-permute-start.2) | collective-permute-done | bytes 127008 | tf_op jit(solution)/shard_map/ppermute | solution.py:289
  14.6 0.1 add_convert_fusion
  14.7 0.5 %collective-permute-start.5 = (bf16[496,128]{1,0:T(8,128)(2,1)S(1)}, bf16[496,128]{1,0:T(8,128)(2,1)S(1)}, u32[]{:S(2)}, u32[]{:S(2)}) collective-permute-start(bf16[496,128]{1,0:T(8,128)(2,1)S(1)} %add_convert_fusion), channel_id=1, source_target_pairs={{0,12},{2,14},{4,8},{6,10},{8,4},{10,6},{12,0},{14,2},{1,13},{3,15... | collective-permute-start | bytes 380936 | tf_op jit(solution)/shard_map/ppermute | solution.py:289
  15.2 1.8 %query.1 = (bf16[5,256,128]{2,1,0:T(8,128)(2,1)S(1)}, f32[5,256,128]{2,1,0:T(8,128)S(1)}, f32[5,256,128]{2,1,0:T(8,128)S(1)}, bf16[256,560]{1,0:T(8,128)(2,1)}) custom-call(s32[1]{0:T(128)} %bitcast.row_ref, s32[1]{0:T(128)} %bitcast.1.place_ref, bf16[5,256,128]{2,1,0:T(8,128)(2,1)S(1)} %get-tuple-element.28.mixed_ref, ...), custom_call_target="tpu_custom_call" | custom-call | flops 167772160 | bytes 3624968 | tf_op jit(solution)/shard_map/query/pallas_call | solution.py:22
  17.0 5.3 %collective-permute-done.5.got_ref = bf16[496,128]{1,0:T(8,128)(2,1)S(1)} collective-permute-done((bf16[496,128]{1,0:T(8,128)(2,1)S(1)}, bf16[496,128]{1,0:T(8,128)(2,1)S(1)}, u32[]{:S(2)}, u32[]{:S(2)}) %collective-permute-start.5) | collective-permute-done | bytes 127008 | tf_op jit(solution)/shard_map/ppermute | solution.py:289
  22.4 1.3 %finish.1 = bf16[256,560]{1,0:T(8,128)(2,1)} custom-call(s32[1]{0:T(128)} %bitcast.row_ref, s32[1]{0:T(128)} %bitcast.1.place_ref, bf16[5,256,128]{2,1,0:T(8,128)(2,1)S(1)} %get-tuple-element.28.mixed_ref, bf16[5,256,128]{2,1,0:T(8,128)(2,1)S(1)} %get-tuple-element.35.q_ref, ...), custom_call_target="tpu_custom_call", output_to_operand_aliasing={{}: (7, {})} | custom-call | flops 41943040 | bytes 2666504 | tf_op jit(solution)/shard_map/finish/pallas_call | solution.py:22
Async XLA Ops:
  0.0 1.8 %collective-permute-start = (bf16[128,1120]{1,0:T(8,128)(2,1)}, bf16[128,1120]{1,0:T(8,128)(2,1)S(1)}, u32[]{:S(2)}, u32[]{:S(2)}) collective-permute-start(bf16[128,1120]{1,0:T(8,128)(2,1)} %bitcast.4), channel_id=1, source_target_pairs={{0,1},{1,0},{2,3},{3,2},{4,5},{5,4},{6,7},{7,6},{8,9},{9,8},{10,11... | collective-permute-start | bytes 860168 | tf_op jit(solution)/shard_map/ppermute | solution.py:331
  1.6 1.9 %copy-start = (bf16[4,10,112,112]{3,2,1,0:T(8,128)(2,1)S(1)}, bf16[4,10,112,112]{3,2,1,0:T(8,128)(2,1)}, u32[]{:S(2)}) copy-start(bf16[4,10,112,112]{3,2,1,0:T(8,128)(2,1)} %w_ref.1) | copy-start | bytes 3010564
  3.0 1.4 %collective-permute-start.1 = (f32[8,128]{1,0:T(8,128)S(1)}, f32[8,128]{1,0:T(8,128)S(1)}, u32[]{:S(2)}, u32[]{:S(2)}) collective-permute-start(f32[8,128]{1,0:T(8,128)S(1)} %get-tuple-element.29.part_ref), channel_id=1, source_target_pairs={{0,1},{1,0},{2,3},{3,2},{4,5},{5,4},{6,7},{7,6},{8,9},{9,8},{10,11... | collective-permute-start | bytes 12296 | tf_op jit(solution)/shard_map/ppermute | solution.py:345
  4.9 5.7 %collective-permute-start.4 = (bf16[496,128]{1,0:T(8,128)(2,1)S(1)}, bf16[496,128]{1,0:T(8,128)(2,1)S(1)}, u32[]{:S(2)}, u32[]{:S(2)}) collective-permute-start(bf16[496,128]{1,0:T(8,128)(2,1)S(1)} %get-tuple-element.34), channel_id=1, source_target_pairs={{0,2},{2,0},{4,6},{6,4},{8,10},{10,8},{12,14},{14,12},{1,3},{3,1},... | collective-permute-start | bytes 380936 | tf_op jit(solution)/shard_map/ppermute | solution.py:289
  6.5 6.3 %collective-permute-start.3 = (bf16[496,128]{1,0:T(8,128)(2,1)S(1)}, bf16[496,128]{1,0:T(8,128)(2,1)S(1)}, u32[]{:S(2)}, u32[]{:S(2)}) collective-permute-start(bf16[496,128]{1,0:T(8,128)(2,1)S(1)} %get-tuple-element.34), channel_id=1, source_target_pairs={{0,4},{2,6},{4,0},{6,2},{8,12},{10,14},{12,8},{14,10},{1,5},{3,7},... | collective-permute-start | bytes 380936 | tf_op jit(solution)/shard_map/ppermute | solution.py:289
  8.1 6.5 %collective-permute-start.2 = (bf16[496,128]{1,0:T(8,128)(2,1)S(1)}, bf16[496,128]{1,0:T(8,128)(2,1)S(1)}, u32[]{:S(2)}, u32[]{:S(2)}) collective-permute-start(bf16[496,128]{1,0:T(8,128)(2,1)S(1)} %get-tuple-element.34), channel_id=1, source_target_pairs={{0,6},{2,4},{4,2},{6,0},{8,14},{10,12},{12,10},{14,8},{1,7},{3,5},... | collective-permute-start | bytes 380936 | tf_op jit(solution)/shard_map/ppermute | solution.py:289
  14.7 7.7 %collective-permute-start.5 = (bf16[496,128]{1,0:T(8,128)(2,1)S(1)}, bf16[496,128]{1,0:T(8,128)(2,1)S(1)}, u32[]{:S(2)}, u32[]{:S(2)}) collective-permute-start(bf16[496,128]{1,0:T(8,128)(2,1)S(1)} %add_convert_fusion), channel_id=1, source_target_pairs={{0,12},{2,14},{4,8},{6,10},{8,4},{10,6},{12,0},{14,2},{1,13},{3,15... | collective-permute-start | bytes 380936 | tf_op jit(solution)/shard_map/ppermute | solution.py:289

commit v7 on v6

--- a/solution.py
+++ b/solution.py
@@ -161,13 +161,14 @@
     for h in range(heads):
         mapped = jnp.dot(mixed_ref[h], maps_ref[h, :, LANES : 3 * LANES], preferred_element_type=F32)
         k_ref[h] = jnp.maximum(mapped[:, :LANES], 0.0)
-        v_ref[h] = mapped[:, LANES:]
+        v_ref[h] = mapped[:, LANES:].astype(BF16)
 
 
 def state_kernel(heads, dim, width, k_ref, v_ref, part_ref, got_ref, state_ref, sent_ref):
     inv = token_scale(width, k_ref.shape[1] // SUBLANES, part_ref, got_ref)
-    for h in range(heads):
-        state = outer_sum((k_ref[h] * inv).astype(BF16), (v_ref[h] * inv).astype(BF16))
+    square = inv * inv
+    for h in range(heads):
+        state = outer_sum((k_ref[h] * square).astype(BF16), v_ref[h])
         state_ref[h] = state
         store_packed(sent_ref, h, heads, dim, state[:dim].astype(BF16))
 
@@ -345,7 +346,7 @@
     got_part = lax.ppermute(part, "row", swap)
     maps_c, k, v = call(
         functools.partial(early_kernel, heads), "early",
-        [packed_maps] + [shape(heads, tokens, LANES, kind=F32)] * 2,
+        [packed_maps, shape(heads, tokens, LANES, kind=F32), shape(heads, tokens, LANES)],
         [row, mixed, causal_weights], [SMEM, VMEM, VMEM], flops=head_flops * 2,
     )
     state, sent = call(

time: 23.8 us -> 23.8 us (level)
  no operation moved by 1% of the time
where the time goes in v7:
time: 23.8 us; the launch traced here: 23.6 us
  waiting for transfers between devices  12 us (50%)
  Pallas kernels  6.91 us (29%)
  starting transfers between devices  4.61 us (19%)
    ppermute x4, waiting for transfers between devices, exchange_rounds(): lax.ppermute(sent, axis, [(i, i ^ mask) for i in range(size)])  11.4 us
    pallas_call x6, Pallas kernels, call(): pl.pallas_call(kernel, name=name, out_shape=tuple(outs), in_specs=in_spec...  6.91 us
    ppermute x4, starting transfers between devices, exchange_rounds(): lax.ppermute(sent, axis, [(i, i ^ mask) for i in range(size)])  4.07 us
    ppermute x1, starting transfers between devices, body(): got_part = lax.ppermute(part, 'row', swap)  0.53 us
  transfers between devices with their start and end apart: 6, of which 6 were waited for; matrix products, arithmetic and copies ran while one was open for 0% of the time, Pallas kernels for 16%

profile of v7, /device:TPU:20, one launch (start us, length us, event | category | flops | bytes accessed | tf_op | source)
XLA Modules:
  0.0 23.6 jit_solution(3367136718548507409)
XLA Ops:
  0.0 0.0 collective-permute-start
  0.0 1.6 %lead.1 = (bf16[5,128,128]{2,1,0:T(8,128)(2,1)S(1)}, bf16[5,128,128]{2,1,0:T(8,128)(2,1)S(1)}, bf16[5,128,128]{2,1,0:T(8,128)(2,1)S(1)}, bf16[5,128,128]{2,1,0:T...) custom-call(s32[1]{0:T(128)} %bitcast.row_ref, bf16[128,1120]{1,0:T(8,128)(2,1)} %bitcast.5, ...), custom_call_target="tpu_custom_call" | custom-call | flops 83886080 | bytes 2928644 | tf_op jit(solution)/shard_map/lead/pallas_call | solution.py:22
  1.6 0.0 copy-start
  1.7 0.1 collective-permute-done.other_ref
  1.8 1.2 %spatial.1 = (bf16[5,256,128]{2,1,0:T(8,128)(2,1)S(1)}, f32[8,128]{1,0:T(8,128)S(1)}) custom-call(s32[1]{0:T(128)} %bitcast.row_ref, bf16[5,128,128]{2,1,0:T(8,128)(2,1)S(1)} %get-tuple-element.22.x_own_ref, bf16[5,128,128]{2,1,0:T(8,128)(2,1)S(1)} %get-tuple-element.23.q_own_ref, bf16[5,128,128]{2,1,0:T(8,128)(2,1)S(1)} %get-tuple-element.24.k_own_ref, ...), custom_call_target="tpu_custom_call" | custom-call | flops 167772160 | bytes 2256900 | tf_op jit(solution)/shard_map/spatial/pallas_call | solution.py:22
  3.0 0.5 %collective-permute-start.1 = (f32[8,128]{1,0:T(8,128)S(1)}, f32[8,128]{1,0:T(8,128)S(1)}, u32[]{:S(2)}, u32[]{:S(2)}) collective-permute-start(f32[8,128]{1,0:T(8,128)S(1)} %get-tuple-element.29.part_ref), channel_id=1, source_target_pairs={{0,1},{1,0},{2,3},{3,2},{4,5},{5,4},{6,7},{7,6},{8,9},{9,8},{10,11... | collective-permute-start | bytes 12296 | tf_op jit(solution)/shard_map/ppermute | solution.py:346
  3.6 0.0 copy-done
  3.6 0.4 %early.1 = (bf16[5,128,512]{2,1,0:T(8,128)(2,1)S(1)}, f32[5,256,128]{2,1,0:T(8,128)S(1)}, bf16[5,256,128]{2,1,0:T(8,128)(2,1)S(1)}) custom-call(s32[1]{0:T(128)} %bitcast.row_ref, bf16[5,256,128]{2,1,0:T(8,128)(2,1)S(1)} %get-tuple-element.28.mixed_ref, bf16[4,10,112,112]{3,2,1,0:T(8,128)(2,1)S(1)} %copy-done), custom_call_target="tpu_custom_call" | custom-call | flops 83886080 | bytes 2969604 | tf_op jit(solution)/shard_map/early/pallas_call | solution.py:22
  4.0 0.4 %collective-permute-done.1.got_ref.got_part_ref = f32[8,128]{1,0:T(8,128)S(1)} collective-permute-done((f32[8,128]{1,0:T(8,128)S(1)}, f32[8,128]{1,0:T(8,128)S(1)}, u32[]{:S(2)}, u32[]{:S(2)}) %collective-permute-start.1) | collective-permute-done | bytes 4128 | tf_op jit(solution)/shard_map/ppermute | solution.py:346
  4.4 0.6 %state.1 = (f32[5,128,128]{2,1,0:T(8,128)S(1)}, bf16[496,128]{1,0:T(8,128)(2,1)S(1)}) custom-call(f32[5,256,128]{2,1,0:T(8,128)S(1)} %get-tuple-element.31.k_ref, bf16[5,256,128]{2,1,0:T(8,128)(2,1)S(1)} %get-tuple-element.32.v_ref, f32[8,128]{1,0:T(8,128)S(1)} %get-tuple-element.29.part_ref, f32[8,128]{1,0:T(8,128)S(1)} %collective-permute-done.1.got_ref.got_part_ref), custom_call_target="tpu_custom_call" | custom-call | flops 41943040 | bytes 1445888 | tf_op jit(solution)/shard_map/state/pallas_call | solution.py:22
  4.9 1.6 %collective-permute-start.4 = (bf16[496,128]{1,0:T(8,128)(2,1)S(1)}, bf16[496,128]{1,0:T(8,128)(2,1)S(1)}, u32[]{:S(2)}, u32[]{:S(2)}) collective-permute-start(bf16[496,128]{1,0:T(8,128)(2,1)S(1)} %get-tuple-element.34), channel_id=1, source_target_pairs={{0,2},{2,0},{4,6},{6,4},{8,10},{10,8},{12,14},{14,12},{1,3},{3,1},... | collective-permute-start | bytes 380936 | tf_op jit(solution)/shard_map/ppermute | solution.py:290
  6.5 1.6 %collective-permute-start.3 = (bf16[496,128]{1,0:T(8,128)(2,1)S(1)}, bf16[496,128]{1,0:T(8,128)(2,1)S(1)}, u32[]{:S(2)}, u32[]{:S(2)}) collective-permute-start(bf16[496,128]{1,0:T(8,128)(2,1)S(1)} %get-tuple-element.34), channel_id=1, source_target_pairs={{0,4},{2,6},{4,0},{6,2},{8,12},{10,14},{12,8},{14,10},{1,5},{3,7},... | collective-permute-start | bytes 380936 | tf_op jit(solution)/shard_map/ppermute | solution.py:290
  8.1 0.4 %collective-permute-start.2 = (bf16[496,128]{1,0:T(8,128)(2,1)S(1)}, bf16[496,128]{1,0:T(8,128)(2,1)S(1)}, u32[]{:S(2)}, u32[]{:S(2)}) collective-permute-start(bf16[496,128]{1,0:T(8,128)(2,1)S(1)} %get-tuple-element.34), channel_id=1, source_target_pairs={{0,6},{2,4},{4,2},{6,0},{8,14},{10,12},{12,10},{14,8},{1,7},{3,5},... | collective-permute-start | bytes 380936 | tf_op jit(solution)/shard_map/ppermute | solution.py:290
  8.5 2.2 %collective-permute-done.4.refs_2_ = bf16[496,128]{1,0:T(8,128)(2,1)S(1)} collective-permute-done((bf16[496,128]{1,0:T(8,128)(2,1)S(1)}, bf16[496,128]{1,0:T(8,128)(2,1)S(1)}, u32[]{:S(2)}, u32[]{:S(2)}) %collective-permute-start.4) | collective-permute-done | bytes 127008 | tf_op jit(solution)/shard_map/ppermute | solution.py:290
  10.7 2.1 %collective-permute-done.3.refs_1_ = bf16[496,128]{1,0:T(8,128)(2,1)S(1)} collective-permute-done((bf16[496,128]{1,0:T(8,128)(2,1)S(1)}, bf16[496,128]{1,0:T(8,128)(2,1)S(1)}, u32[]{:S(2)}, u32[]{:S(2)}) %collective-permute-start.3) | collective-permute-done | bytes 127008 | tf_op jit(solution)/shard_map/ppermute | solution.py:290
  12.8 1.8 %collective-permute-done.2.refs_0_ = bf16[496,128]{1,0:T(8,128)(2,1)S(1)} collective-permute-done((bf16[496,128]{1,0:T(8,128)(2,1)S(1)}, bf16[496,128]{1,0:T(8,128)(2,1)S(1)}, u32[]{:S(2)}, u32[]{:S(2)}) %collective-permute-start.2) | collective-permute-done | bytes 127008 | tf_op jit(solution)/shard_map/ppermute | solution.py:290
  14.6 0.1 add_convert_fusion
  14.6 0.5 %collective-permute-start.5 = (bf16[496,128]{1,0:T(8,128)(2,1)S(1)}, bf16[496,128]{1,0:T(8,128)(2,1)S(1)}, u32[]{:S(2)}, u32[]{:S(2)}) collective-permute-start(bf16[496,128]{1,0:T(8,128)(2,1)S(1)} %add_convert_fusion), channel_id=1, source_target_pairs={{0,12},{2,14},{4,8},{6,10},{8,4},{10,6},{12,0},{14,2},{1,13},{3,15... | collective-permute-start | bytes 380936 | tf_op jit(solution)/shard_map/ppermute | solution.py:290
  15.2 1.9 %query.1 = (bf16[5,256,128]{2,1,0:T(8,128)(2,1)S(1)}, f32[5,256,128]{2,1,0:T(8,128)S(1)}, f32[5,256,128]{2,1,0:T(8,128)S(1)}, bf16[256,560]{1,0:T(8,128)(2,1)}) custom-call(s32[1]{0:T(128)} %bitcast.row_ref, s32[1]{0:T(128)} %bitcast.1.place_ref, bf16[5,256,128]{2,1,0:T(8,128)(2,1)S(1)} %get-tuple-element.28.mixed_ref, ...), custom_call_target="tpu_custom_call" | custom-call | flops 167772160 | bytes 3624968 | tf_op jit(solution)/shard_map/query/pallas_call | solution.py:22
  17.0 5.3 %collective-permute-done.5.got_ref = bf16[496,128]{1,0:T(8,128)(2,1)S(1)} collective-permute-done((bf16[496,128]{1,0:T(8,128)(2,1)S(1)}, bf16[496,128]{1,0:T(8,128)(2,1)S(1)}, u32[]{:S(2)}, u32[]{:S(2)}) %collective-permute-start.5) | collective-permute-done | bytes 127008 | tf_op jit(solution)/shard_map/ppermute | solution.py:290
  22.4 1.3 %finish.1 = bf16[256,560]{1,0:T(8,128)(2,1)} custom-call(s32[1]{0:T(128)} %bitcast.row_ref, s32[1]{0:T(128)} %bitcast.1.place_ref, bf16[5,256,128]{2,1,0:T(8,128)(2,1)S(1)} %get-tuple-element.28.mixed_ref, bf16[5,256,128]{2,1,0:T(8,128)(2,1)S(1)} %get-tuple-element.35.q_ref, ...), custom_call_target="tpu_custom_call", output_to_operand_aliasing={{}: (7, {})} | custom-call | flops 41943040 | bytes 2666504 | tf_op jit(solution)/shard_map/finish/pallas_call | solution.py:22
Async XLA Ops:
  0.0 1.8 %collective-permute-start = (bf16[128,1120]{1,0:T(8,128)(2,1)}, bf16[128,1120]{1,0:T(8,128)(2,1)S(1)}, u32[]{:S(2)}, u32[]{:S(2)}) collective-permute-start(bf16[128,1120]{1,0:T(8,128)(2,1)} %bitcast.4), channel_id=1, source_target_pairs={{0,1},{1,0},{2,3},{3,2},{4,5},{5,4},{6,7},{7,6},{8,9},{9,8},{10,11... | collective-permute-start | bytes 860168 | tf_op jit(solution)/shard_map/ppermute | solution.py:332
  1.6 1.9 %copy-start = (bf16[4,10,112,112]{3,2,1,0:T(8,128)(2,1)S(1)}, bf16[4,10,112,112]{3,2,1,0:T(8,128)(2,1)}, u32[]{:S(2)}) copy-start(bf16[4,10,112,112]{3,2,1,0:T(8,128)(2,1)} %w_ref.1) | copy-start | bytes 3010564
  3.0 1.4 %collective-permute-start.1 = (f32[8,128]{1,0:T(8,128)S(1)}, f32[8,128]{1,0:T(8,128)S(1)}, u32[]{:S(2)}, u32[]{:S(2)}) collective-permute-start(f32[8,128]{1,0:T(8,128)S(1)} %get-tuple-element.29.part_ref), channel_id=1, source_target_pairs={{0,1},{1,0},{2,3},{3,2},{4,5},{5,4},{6,7},{7,6},{8,9},{9,8},{10,11... | collective-permute-start | bytes 12296 | tf_op jit(solution)/shard_map/ppermute | solution.py:346
  4.9 5.7 %collective-permute-start.4 = (bf16[496,128]{1,0:T(8,128)(2,1)S(1)}, bf16[496,128]{1,0:T(8,128)(2,1)S(1)}, u32[]{:S(2)}, u32[]{:S(2)}) collective-permute-start(bf16[496,128]{1,0:T(8,128)(2,1)S(1)} %get-tuple-element.34), channel_id=1, source_target_pairs={{0,2},{2,0},{4,6},{6,4},{8,10},{10,8},{12,14},{14,12},{1,3},{3,1},... | collective-permute-start | bytes 380936 | tf_op jit(solution)/shard_map/ppermute | solution.py:290
  6.5 6.3 %collective-permute-start.3 = (bf16[496,128]{1,0:T(8,128)(2,1)S(1)}, bf16[496,128]{1,0:T(8,128)(2,1)S(1)}, u32[]{:S(2)}, u32[]{:S(2)}) collective-permute-start(bf16[496,128]{1,0:T(8,128)(2,1)S(1)} %get-tuple-element.34), channel_id=1, source_target_pairs={{0,4},{2,6},{4,0},{6,2},{8,12},{10,14},{12,8},{14,10},{1,5},{3,7},... | collective-permute-start | bytes 380936 | tf_op jit(solution)/shard_map/ppermute | solution.py:290
  8.1 6.5 %collective-permute-start.2 = (bf16[496,128]{1,0:T(8,128)(2,1)S(1)}, bf16[496,128]{1,0:T(8,128)(2,1)S(1)}, u32[]{:S(2)}, u32[]{:S(2)}) collective-permute-start(bf16[496,128]{1,0:T(8,128)(2,1)S(1)} %get-tuple-element.34), channel_id=1, source_target_pairs={{0,6},{2,4},{4,2},{6,0},{8,14},{10,12},{12,10},{14,8},{1,7},{3,5},... | collective-permute-start | bytes 380936 | tf_op jit(solution)/shard_map/ppermute | solution.py:290
  14.6 7.7 %collective-permute-start.5 = (bf16[496,128]{1,0:T(8,128)(2,1)S(1)}, bf16[496,128]{1,0:T(8,128)(2,1)S(1)}, u32[]{:S(2)}, u32[]{:S(2)}) collective-permute-start(bf16[496,128]{1,0:T(8,128)(2,1)S(1)} %add_convert_fusion), channel_id=1, source_target_pairs={{0,12},{2,14},{4,8},{6,10},{8,4},{10,6},{12,0},{14,2},{1,13},{3,15... | collective-permute-start | bytes 380936 | tf_op jit(solution)/shard_map/ppermute | solution.py:290

commit v8 on v6

--- a/solution.py
+++ b/solution.py
@@ -160,14 +160,15 @@
         pack_map(heads, row_ref[0] * heads, m, w_ref, maps_ref)
     for h in range(heads):
         mapped = jnp.dot(mixed_ref[h], maps_ref[h, :, LANES : 3 * LANES], preferred_element_type=F32)
-        k_ref[h] = jnp.maximum(mapped[:, :LANES], 0.0)
+        k_ref[h] = jnp.maximum(mapped[:, :LANES], 0.0).astype(BF16).T
         v_ref[h] = mapped[:, LANES:]
 
 
 def state_kernel(heads, dim, width, k_ref, v_ref, part_ref, got_ref, state_ref, sent_ref):
-    inv = token_scale(width, k_ref.shape[1] // SUBLANES, part_ref, got_ref)
-    for h in range(heads):
-        state = outer_sum((k_ref[h] * inv).astype(BF16), (v_ref[h] * inv).astype(BF16))
+    inv = token_scale(width, v_ref.shape[1] // SUBLANES, part_ref, got_ref)
+    square = inv * inv
+    for h in range(heads):
+        state = jnp.dot(k_ref[h], (v_ref[h] * square).astype(BF16), preferred_element_type=F32)
         state_ref[h] = state
         store_packed(sent_ref, h, heads, dim, state[:dim].astype(BF16))
 
@@ -345,7 +346,7 @@
     got_part = lax.ppermute(part, "row", swap)
     maps_c, k, v = call(
         functools.partial(early_kernel, heads), "early",
-        [packed_maps] + [shape(heads, tokens, LANES, kind=F32)] * 2,
+        [packed_maps, shape(heads, LANES, tokens), shape(heads, tokens, LANES, kind=F32)],
         [row, mixed, causal_weights], [SMEM, VMEM, VMEM], flops=head_flops * 2,
     )
     state, sent = call(

time: 23.8 us -> 23.7 us (level)
  transfers between devices with their start and end apart: 6 -> 6, of which waited for: 6 -> 6; matrix products, arithmetic and copies ran while one was open for 0% -> 0% of each run, Pallas kernels for 16% -> 17%
where the time goes in v8:
time: 23.7 us; the launch traced here: 23.6 us
  waiting for transfers between devices  11.9 us (50%)
  Pallas kernels  6.96 us (29%)
  starting transfers between devices  4.6 us (19%)
    ppermute x4, waiting for transfers between devices, exchange_rounds(): lax.ppermute(sent, axis, [(i, i ^ mask) for i in range(size)])  11.4 us
    pallas_call x6, Pallas kernels, call(): pl.pallas_call(kernel, name=name, out_shape=tuple(outs), in_specs=in_spec...  6.96 us
    ppermute x4, starting transfers between devices, exchange_rounds(): lax.ppermute(sent, axis, [(i, i ^ mask) for i in range(size)])  4.07 us
    ppermute x1, starting transfers between devices, body(): got_part = lax.ppermute(part, 'row', swap)  0.53 us
  transfers between devices with their start and end apart: 6, of which 6 were waited for; matrix products, arithmetic and copies ran while one was open for 0% of the time, Pallas kernels for 17%

profile of v8, /device:TPU:20, one launch (start us, length us, event | category | flops | bytes accessed | tf_op | source)
XLA Modules:
  0.0 23.6 jit_solution(17851997817652797932)
XLA Ops:
  0.0 0.0 collective-permute-start
  0.0 1.6 %lead.1 = (bf16[5,128,128]{2,1,0:T(8,128)(2,1)S(1)}, bf16[5,128,128]{2,1,0:T(8,128)(2,1)S(1)}, bf16[5,128,128]{2,1,0:T(8,128)(2,1)S(1)}, bf16[5,128,128]{2,1,0:T...) custom-call(s32[1]{0:T(128)} %bitcast.row_ref, bf16[128,1120]{1,0:T(8,128)(2,1)} %bitcast.5, ...), custom_call_target="tpu_custom_call" | custom-call | flops 83886080 | bytes 2928644 | tf_op jit(solution)/shard_map/lead/pallas_call | solution.py:22
  1.6 0.0 copy-start
  1.7 0.1 collective-permute-done.other_ref
  1.8 1.2 %spatial.1 = (bf16[5,256,128]{2,1,0:T(8,128)(2,1)S(1)}, f32[8,128]{1,0:T(8,128)S(1)}) custom-call(s32[1]{0:T(128)} %bitcast.row_ref, bf16[5,128,128]{2,1,0:T(8,128)(2,1)S(1)} %get-tuple-element.22.x_own_ref, bf16[5,128,128]{2,1,0:T(8,128)(2,1)S(1)} %get-tuple-element.23.q_own_ref, bf16[5,128,128]{2,1,0:T(8,128)(2,1)S(1)} %get-tuple-element.24.k_own_ref, ...), custom_call_target="tpu_custom_call" | custom-call | flops 167772160 | bytes 2256900 | tf_op jit(solution)/shard_map/spatial/pallas_call | solution.py:22
  3.0 0.5 %collective-permute-start.1 = (f32[8,128]{1,0:T(8,128)S(1)}, f32[8,128]{1,0:T(8,128)S(1)}, u32[]{:S(2)}, u32[]{:S(2)}) collective-permute-start(f32[8,128]{1,0:T(8,128)S(1)} %get-tuple-element.29.part_ref), channel_id=1, source_target_pairs={{0,1},{1,0},{2,3},{3,2},{4,5},{5,4},{6,7},{7,6},{8,9},{9,8},{10,11... | collective-permute-start | bytes 12296 | tf_op jit(solution)/shard_map/ppermute | solution.py:346
  3.6 0.0 copy-done
  3.6 0.5 %early.1 = (bf16[5,128,512]{2,1,0:T(8,128)(2,1)S(1)}, bf16[5,128,256]{2,1,0:T(8,128)(2,1)S(1)}, f32[5,256,128]{2,1,0:T(8,128)S(1)}) custom-call(s32[1]{0:T(128)} %bitcast.row_ref, bf16[5,256,128]{2,1,0:T(8,128)(2,1)S(1)} %get-tuple-element.28.mixed_ref, bf16[4,10,112,112]{3,2,1,0:T(8,128)(2,1)S(1)} %copy-done), custom_call_target="tpu_custom_call" | custom-call | flops 83886080 | bytes 2969604 | tf_op jit(solution)/shard_map/early/pallas_call | solution.py:22
  4.0 0.4 %collective-permute-done.1.got_ref.got_part_ref = f32[8,128]{1,0:T(8,128)S(1)} collective-permute-done((f32[8,128]{1,0:T(8,128)S(1)}, f32[8,128]{1,0:T(8,128)S(1)}, u32[]{:S(2)}, u32[]{:S(2)}) %collective-permute-start.1) | collective-permute-done | bytes 4128 | tf_op jit(solution)/shard_map/ppermute | solution.py:346
  4.4 0.5 %state.1 = (f32[5,128,128]{2,1,0:T(8,128)S(1)}, bf16[496,128]{1,0:T(8,128)(2,1)S(1)}) custom-call(bf16[5,128,256]{2,1,0:T(8,128)(2,1)S(1)} %get-tuple-element.31.k_ref, f32[5,256,128]{2,1,0:T(8,128)S(1)} %get-tuple-element.32.v_ref, f32[8,128]{1,0:T(8,128)S(1)} %get-tuple-element.29.part_ref, f32[8,128]{1,0:T(8,128)S(1)} %collective-permute-done.1.got_ref.got_part_ref), custom_call_target="tpu_custom_call" | custom-call | flops 41943040 | bytes 1445888 | tf_op jit(solution)/shard_map/state/pallas_call | solution.py:22
  4.9 1.6 %collective-permute-start.4 = (bf16[496,128]{1,0:T(8,128)(2,1)S(1)}, bf16[496,128]{1,0:T(8,128)(2,1)S(1)}, u32[]{:S(2)}, u32[]{:S(2)}) collective-permute-start(bf16[496,128]{1,0:T(8,128)(2,1)S(1)} %get-tuple-element.34), channel_id=1, source_target_pairs={{0,2},{2,0},{4,6},{6,4},{8,10},{10,8},{12,14},{14,12},{1,3},{3,1},... | collective-permute-start | bytes 380936 | tf_op jit(solution)/shard_map/ppermute | solution.py:290
  6.5 1.6 %collective-permute-start.3 = (bf16[496,128]{1,0:T(8,128)(2,1)S(1)}, bf16[496,128]{1,0:T(8,128)(2,1)S(1)}, u32[]{:S(2)}, u32[]{:S(2)}) collective-permute-start(bf16[496,128]{1,0:T(8,128)(2,1)S(1)} %get-tuple-element.34), channel_id=1, source_target_pairs={{0,4},{2,6},{4,0},{6,2},{8,12},{10,14},{12,8},{14,10},{1,5},{3,7},... | collective-permute-start | bytes 380936 | tf_op jit(solution)/shard_map/ppermute | solution.py:290
  8.1 0.4 %collective-permute-start.2 = (bf16[496,128]{1,0:T(8,128)(2,1)S(1)}, bf16[496,128]{1,0:T(8,128)(2,1)S(1)}, u32[]{:S(2)}, u32[]{:S(2)}) collective-permute-start(bf16[496,128]{1,0:T(8,128)(2,1)S(1)} %get-tuple-element.34), channel_id=1, source_target_pairs={{0,6},{2,4},{4,2},{6,0},{8,14},{10,12},{12,10},{14,8},{1,7},{3,5},... | collective-permute-start | bytes 380936 | tf_op jit(solution)/shard_map/ppermute | solution.py:290
  8.5 2.2 %collective-permute-done.4.refs_2_ = bf16[496,128]{1,0:T(8,128)(2,1)S(1)} collective-permute-done((bf16[496,128]{1,0:T(8,128)(2,1)S(1)}, bf16[496,128]{1,0:T(8,128)(2,1)S(1)}, u32[]{:S(2)}, u32[]{:S(2)}) %collective-permute-start.4) | collective-permute-done | bytes 127008 | tf_op jit(solution)/shard_map/ppermute | solution.py:290
  10.6 2.1 %collective-permute-done.3.refs_1_ = bf16[496,128]{1,0:T(8,128)(2,1)S(1)} collective-permute-done((bf16[496,128]{1,0:T(8,128)(2,1)S(1)}, bf16[496,128]{1,0:T(8,128)(2,1)S(1)}, u32[]{:S(2)}, u32[]{:S(2)}) %collective-permute-start.3) | collective-permute-done | bytes 127008 | tf_op jit(solution)/shard_map/ppermute | solution.py:290
  12.8 1.8 %collective-permute-done.2.refs_0_ = bf16[496,128]{1,0:T(8,128)(2,1)S(1)} collective-permute-done((bf16[496,128]{1,0:T(8,128)(2,1)S(1)}, bf16[496,128]{1,0:T(8,128)(2,1)S(1)}, u32[]{:S(2)}, u32[]{:S(2)}) %collective-permute-start.2) | collective-permute-done | bytes 127008 | tf_op jit(solution)/shard_map/ppermute | solution.py:290
  14.5 0.1 add_convert_fusion
  14.6 0.5 %collective-permute-start.5 = (bf16[496,128]{1,0:T(8,128)(2,1)S(1)}, bf16[496,128]{1,0:T(8,128)(2,1)S(1)}, u32[]{:S(2)}, u32[]{:S(2)}) collective-permute-start(bf16[496,128]{1,0:T(8,128)(2,1)S(1)} %add_convert_fusion), channel_id=1, source_target_pairs={{0,12},{2,14},{4,8},{6,10},{8,4},{10,6},{12,0},{14,2},{1,13},{3,15... | collective-permute-start | bytes 380936 | tf_op jit(solution)/shard_map/ppermute | solution.py:290
  15.1 1.9 %query.1 = (bf16[5,256,128]{2,1,0:T(8,128)(2,1)S(1)}, f32[5,256,128]{2,1,0:T(8,128)S(1)}, f32[5,256,128]{2,1,0:T(8,128)S(1)}, bf16[256,560]{1,0:T(8,128)(2,1)}) custom-call(s32[1]{0:T(128)} %bitcast.row_ref, s32[1]{0:T(128)} %bitcast.1.place_ref, bf16[5,256,128]{2,1,0:T(8,128)(2,1)S(1)} %get-tuple-element.28.mixed_ref, ...), custom_call_target="tpu_custom_call" | custom-call | flops 167772160 | bytes 3624968 | tf_op jit(solution)/shard_map/query/pallas_call | solution.py:22
  17.0 5.3 %collective-permute-done.5.got_ref = bf16[496,128]{1,0:T(8,128)(2,1)S(1)} collective-permute-done((bf16[496,128]{1,0:T(8,128)(2,1)S(1)}, bf16[496,128]{1,0:T(8,128)(2,1)S(1)}, u32[]{:S(2)}, u32[]{:S(2)}) %collective-permute-start.5) | collective-permute-done | bytes 127008 | tf_op jit(solution)/shard_map/ppermute | solution.py:290
  22.3 1.3 %finish.1 = bf16[256,560]{1,0:T(8,128)(2,1)} custom-call(s32[1]{0:T(128)} %bitcast.row_ref, s32[1]{0:T(128)} %bitcast.1.place_ref, bf16[5,256,128]{2,1,0:T(8,128)(2,1)S(1)} %get-tuple-element.28.mixed_ref, bf16[5,256,128]{2,1,0:T(8,128)(2,1)S(1)} %get-tuple-element.35.q_ref, ...), custom_call_target="tpu_custom_call", output_to_operand_aliasing={{}: (7, {})} | custom-call | flops 41943040 | bytes 2666504 | tf_op jit(solution)/shard_map/finish/pallas_call | solution.py:22
Async XLA Ops:
  0.0 1.8 %collective-permute-start = (bf16[128,1120]{1,0:T(8,128)(2,1)}, bf16[128,1120]{1,0:T(8,128)(2,1)S(1)}, u32[]{:S(2)}, u32[]{:S(2)}) collective-permute-start(bf16[128,1120]{1,0:T(8,128)(2,1)} %bitcast.4), channel_id=1, source_target_pairs={{0,1},{1,0},{2,3},{3,2},{4,5},{5,4},{6,7},{7,6},{8,9},{9,8},{10,11... | collective-permute-start | bytes 860168 | tf_op jit(solution)/shard_map/ppermute | solution.py:332
  1.6 1.9 %copy-start = (bf16[4,10,112,112]{3,2,1,0:T(8,128)(2,1)S(1)}, bf16[4,10,112,112]{3,2,1,0:T(8,128)(2,1)}, u32[]{:S(2)}) copy-start(bf16[4,10,112,112]{3,2,1,0:T(8,128)(2,1)} %w_ref.1) | copy-start | bytes 3010564
  3.0 1.4 %collective-permute-start.1 = (f32[8,128]{1,0:T(8,128)S(1)}, f32[8,128]{1,0:T(8,128)S(1)}, u32[]{:S(2)}, u32[]{:S(2)}) collective-permute-start(f32[8,128]{1,0:T(8,128)S(1)} %get-tuple-element.29.part_ref), channel_id=1, source_target_pairs={{0,1},{1,0},{2,3},{3,2},{4,5},{5,4},{6,7},{7,6},{8,9},{9,8},{10,11... | collective-permute-start | bytes 12296 | tf_op jit(solution)/shard_map/ppermute | solution.py:346
  4.9 5.7 %collective-permute-start.4 = (bf16[496,128]{1,0:T(8,128)(2,1)S(1)}, bf16[496,128]{1,0:T(8,128)(2,1)S(1)}, u32[]{:S(2)}, u32[]{:S(2)}) collective-permute-start(bf16[496,128]{1,0:T(8,128)(2,1)S(1)} %get-tuple-element.34), channel_id=1, source_target_pairs={{0,2},{2,0},{4,6},{6,4},{8,10},{10,8},{12,14},{14,12},{1,3},{3,1},... | collective-permute-start | bytes 380936 | tf_op jit(solution)/shard_map/ppermute | solution.py:290
  6.5 6.3 %collective-permute-start.3 = (bf16[496,128]{1,0:T(8,128)(2,1)S(1)}, bf16[496,128]{1,0:T(8,128)(2,1)S(1)}, u32[]{:S(2)}, u32[]{:S(2)}) collective-permute-start(bf16[496,128]{1,0:T(8,128)(2,1)S(1)} %get-tuple-element.34), channel_id=1, source_target_pairs={{0,4},{2,6},{4,0},{6,2},{8,12},{10,14},{12,8},{14,10},{1,5},{3,7},... | collective-permute-start | bytes 380936 | tf_op jit(solution)/shard_map/ppermute | solution.py:290
  8.1 6.5 %collective-permute-start.2 = (bf16[496,128]{1,0:T(8,128)(2,1)S(1)}, bf16[496,128]{1,0:T(8,128)(2,1)S(1)}, u32[]{:S(2)}, u32[]{:S(2)}) collective-permute-start(bf16[496,128]{1,0:T(8,128)(2,1)S(1)} %get-tuple-element.34), channel_id=1, source_target_pairs={{0,6},{2,4},{4,2},{6,0},{8,14},{10,12},{12,10},{14,8},{1,7},{3,5},... | collective-permute-start | bytes 380936 | tf_op jit(solution)/shard_map/ppermute | solution.py:290
  14.6 7.7 %collective-permute-start.5 = (bf16[496,128]{1,0:T(8,128)(2,1)S(1)}, bf16[496,128]{1,0:T(8,128)(2,1)S(1)}, u32[]{:S(2)}, u32[]{:S(2)}) collective-permute-start(bf16[496,128]{1,0:T(8,128)(2,1)S(1)} %add_convert_fusion), channel_id=1, source_target_pairs={{0,12},{2,14},{4,8},{6,10},{8,4},{10,6},{12,0},{14,2},{1,13},{3,15... | collective-permute-start | bytes 380936 | tf_op jit(solution)/shard_map/ppermute | solution.py:290
